TPU v7x, 32 devices: a whole 2x2x4 slice. The times are simulated.
32 devices in a mesh: row: 4 (over y, x), col: 8 (over z, core).
Axes of the slice: x: 2, y: 2, z: 4, core: 2. Of those that a mesh axis runs over, the one named last changes fastest.
Arguments:
- homolog_stack: bfloat16 [128, 128, 256], P(('row', 'col')), may hold values from -6 to 6
- per_amino_features: bfloat16 [128, 256], P(('row', 'col')), may hold values from -6 to 6
- asking_matrix: bfloat16 [256, 256], replicated, may hold values from -24 to 24
- lookup_matrix: bfloat16 [256, 256], replicated, may hold values from -0.375 to 0.375
- content_matrix: bfloat16 [256, 256], replicated, may hold values from -0.375 to 0.375
- sigmoid_scaling_matrix: bfloat16 [256, 256], replicated, may hold values from -0.375 to 0.375
- attention_result_matrix: bfloat16 [256, 256], replicated, may hold values from -0.375 to 0.375
- stack_transition_expand_matrix: bfloat16 [256, 1024], replicated, may hold values from -0.375 to 0.375
- stack_transition_shrink_matrix: bfloat16 [1024, 256], replicated, may hold values from -0.1875 to 0.1875
- former_factor_matrix: bfloat16 [256, 32], replicated, may hold values from -0.375 to 0.375
- latter_factor_matrix: bfloat16 [256, 32], replicated, may hold values from -0.375 to 0.375
- factor_mean_projection: bfloat16 [1024, 128], replicated, may hold values from -1.1953125 to 1.1953125
- row_amino_embedding: bfloat16 [256, 128], replicated, may hold values from -0.375 to 0.375
- column_amino_embedding: bfloat16 [256, 128], replicated, may hold values from -0.375 to 0.375
- offset_embedding_matrix: bfloat16 [65, 128], replicated, may hold values from -3 to 3
- grid_transition_expand: bfloat16 [128, 512], replicated, may hold values from -0.5 to 0.5
- grid_transition_shrink: bfloat16 [512, 128], replicated, may hold values from -0.25 to 0.25
- distance_bins_matrix: bfloat16 [128, 64], replicated, may hold values from -0.5 to 0.5
Outputs:
- alignment_output: bfloat16 [128, 128, 256], P(None, ('row', 'col'))
- pair_output: bfloat16 [128, 128, 128], P('row', 'col')
- distogram: bfloat16 [128, 128, 64], P('row', 'col')
All inputs are finite; a program needn't handle non-finite values.
Results may differ from a plain program's by a relative error of at most 0.011.
The roundings to bfloat16 on the way count: a program that leaves them out, or rounds other values in their place, can miss the bound.
Values may be sent and summed in bfloat16 or wider, within the bound.
No kernel may reach another device: no remote copies, remote signals or barrier semaphores. Data moves between devices by JAX's collectives and lax.ppermute only.
A program may use at most 256 MiB of HBM per device.

v0:
```python
import functools
import math

import jax
import jax.numpy as jnp
from jax import lax
from jax.experimental import pallas as pl
from jax.experimental.pallas import tpu as pltpu
from jax.sharding import PartitionSpec as P

HEAD = 32
CLIP = 32
LANES = 128
GROUP = 4
SWAP_LIMIT = 512
F32 = jnp.float32
BF16 = jnp.bfloat16


VMEM = pl.BlockSpec(memory_space=pltpu.VMEM)
HBM = pl.BlockSpec(memory_space=pltpu.MemorySpace.HBM)


def near(value):
    return pltpu.with_memory_space_constraint(value, pltpu.MemorySpace.VMEM)


def far(value):
    return pltpu.with_memory_space_constraint(value, pltpu.MemorySpace.HBM)


def local_call(kernel, *, scratch_shapes, **options):
    held = 0
    for ref in jax.tree.leaves(scratch_shapes):
        if ref.memory_space != pltpu.MemorySpace.VMEM:
            continue
        held += math.prod(ref.shape) * jnp.dtype(ref.dtype).itemsize
    limit = min(2 * held + (8 << 20), 48 << 20)
    return pl.pallas_call(
        kernel,
        scratch_shapes=scratch_shapes,
        compiler_params=pltpu.CompilerParams(vmem_limit_bytes=limit),
        **options,
    )


def dot(a, b):
    return jnp.dot(a, b, preferred_element_type=F32)


def standardize(values):
    middle = jnp.mean(values, -1, keepdims=True)
    centred = values - middle
    spread = jnp.mean(centred * centred, -1, keepdims=True)
    return centred * lax.rsqrt(spread + 1e-05)


def for_chunks(count, body):
    if count == 1:
        body(0)
    else:
        lax.fori_loop(0, count, lambda i, carry: (body(i), carry)[1], 0)


def rows_at(start, size):
    if not isinstance(start, int):
        start = pl.multiple_of(start, math.gcd(size, 128))
    return pl.ds(start, size)


def chunk_kernel(n_res, parts, x_far, o_far, x_in, o_out, came, left):
    n_seq, amino, feature = x_far.shape
    width = amino // parts
    rows = n_seq * width
    pair = 2 * n_res
    ins, outs = [], []
    for p in range(parts):
        ins.append(
            pltpu.make_async_copy(x_far.at[:, pl.ds(p * width, width), :], x_in.at[p], came.at[p])
        )
        ins[p].start()
    for p in range(parts):
        ins[p].wait()
        values = [
            x_in[p, seq].astype(F32).reshape(width // pair, pair, feature) for seq in range(n_seq)
        ]
        upper = lax.broadcasted_iota(jnp.int32, values[0].shape, 1) < n_res
        even, odd = [], []
        for seq in range(0, n_seq, 2):
            one, two = values[seq], values[seq + 1]
            even.append(jnp.where(upper, one, pltpu.roll(two, n_res, 1)))
            odd.append(jnp.where(upper, pltpu.roll(one, n_res, 1), two))
        made = jnp.stack(even + odd, axis=1).reshape(rows, feature)
        o_out[p * rows : (p + 1) * rows, :] = made.astype(BF16)
        part = pl.ds(p * rows, rows)
        outs.append(pltpu.make_async_copy(o_out.at[part], o_far.at[part], left.at[p]))
        outs[p].start()
    for copy in outs:
        copy.wait()


def chunks(x, n_res):
    n_seq, amino, feature = x.shape
    parts = 4
    width = amino // parts
    assert n_seq % 2 == 0 and 2 * n_res == 8
    return local_call(
        functools.partial(chunk_kernel, n_res, parts),
        out_shape=pltpu.HBM((n_seq * amino, feature), BF16),
        in_specs=[HBM],
        out_specs=HBM,
        scratch_shapes=[
            pltpu.VMEM((parts, n_seq, width, feature), BF16),
            pltpu.VMEM((n_seq * amino, feature), BF16),
            pltpu.SemaphoreType.DMA((parts,)),
            pltpu.SemaphoreType.DMA((parts,)),
        ],
        name="chunks",
    )(far(x))


def turn_kernel(w_ref, o_ref, w_scr):
    factor = math.isqrt(w_ref.shape[0])
    w_scr[...] = w_ref[...].astype(F32)
    for e in range(factor):
        o_ref[e * factor : (e + 1) * factor, :] = w_scr[pl.ds(e, factor, stride=factor), :].astype(
            BF16
        )


def turn_projection(w):
    return local_call(
        turn_kernel,
        out_shape=pltpu.HBM(w.shape, BF16),
        in_specs=[VMEM],
        out_specs=VMEM,
        scratch_shapes=[pltpu.VMEM(w.shape, F32)],
        name="turn",
    )(w)


def attention_kernel(
    n_res,
    x_ref,
    amino_ref,
    wq_ref,
    wk_ref,
    wv_ref,
    wg_ref,
    wo_ref,
    fg_ref,
    re_ref,
    ce_ref,
    w1_far,
    w2_far,
    _,
    _2,
    align_ref,
    send_ref,
    nat_scr,
    res_scr,
    q_scr,
    k_scr,
    v_scr,
    g_scr,
    mix_scr,
    ln_scr,
    w1_ref,
    w2_ref,
    arrived,
):
    fetch_1 = pltpu.make_async_copy(w1_far, w1_ref, arrived.at[0])
    fetch_2 = pltpu.make_async_copy(w2_far, w2_ref, arrived.at[1])
    fetch_1.start()
    fetch_2.start()
    rows, feature = x_ref.shape
    seqs = rows // n_res
    chunk = min(rows, 512)
    tiles = feature // LANES
    tile_lanes = [slice(t * LANES, (t + 1) * LANES) for t in range(tiles)]
    for t, lanes in enumerate(tile_lanes):
        nat_scr[t] = x_ref[:, lanes].astype(F32)
        for i in range(n_res):
            res_scr[i * seqs : (i + 1) * seqs, lanes] = nat_scr[t, pl.ds(i, seqs, stride=n_res), :]

    def project(step):
        at = rows_at(step * chunk, chunk)
        normed = standardize(res_scr[at, :]).astype(BF16)
        q_scr[at, :] = dot(normed, wq_ref[...]).astype(BF16)
        k_scr[at, :] = dot(normed, wk_ref[...]).astype(BF16)
        v_scr[at, :] = dot(normed, wv_ref[...]).astype(BF16)
        g_scr[at, :] = jax.nn.sigmoid(dot(normed, wg_ref[...]))

    for_chunks(rows // chunk, project)

    group = LANES // HEAD
    head_of_row = lax.broadcasted_iota(jnp.int32, (LANES, seqs), 0) // HEAD
    head_of_lane = lax.broadcasted_iota(jnp.int32, (seqs, LANES), 1) // HEAD
    scale = math.log2(math.e) / math.sqrt(HEAD)

    def attend(index, tile):
        at = rows_at(index * seqs, seqs)
        lanes = tile_lanes[tile]
        q_t = q_scr[at, lanes].astype(F32).T.astype(BF16)
        v_t = v_scr[at, lanes].astype(F32).T
        keys = k_scr[at, lanes].astype(F32)
        stacked = jnp.concatenate(
            [jnp.where(head_of_lane == h, keys, 0.0).astype(BF16) for h in range(group)], axis=0
        )
        scores = dot(stacked, q_t)
        powers, inverse = [], []
        for h in range(group):
            mine = scores[h * seqs : (h + 1) * seqs, :]
            power = jnp.exp2((mine - jnp.max(mine, axis=0, keepdims=True)) * scale)
            total = 1.0 / jnp.sum(power, axis=0, keepdims=True)
            powers.append(power.astype(BF16))
            inverse.append(jnp.broadcast_to(total, (HEAD, seqs)))
        values = jnp.concatenate(
            [jnp.where(head_of_row == h, v_t, 0.0).astype(BF16) for h in range(group)], axis=1
        )
        summed = dot(values, jnp.concatenate(powers, axis=0)) * jnp.concatenate(inverse, axis=0)
        mix_scr[at, lanes] = (summed.T * g_scr[at, lanes]).astype(BF16)

    if seqs <= LANES:
        for i in range(n_res):
            for tile in range(tiles):
                attend(i, tile)
    else:

        def attend_all(i):
            for tile in range(tiles):
                attend(i, tile)

        for_chunks(n_res, attend_all)

    fetch_1.wait()
    fetch_2.wait()

    def transition(step):
        at = rows_at(step * chunk, chunk)
        first = res_scr[at, :] + dot(mix_scr[at, :], wo_ref[...])
        hidden = jnp.maximum(dot(standardize(first).astype(BF16), w1_ref[...]), 0.0).astype(BF16)
        second = first + dot(hidden, w2_ref[...])
        align_ref[at, :] = second.astype(BF16)
        ln_scr[at, :] = standardize(second).astype(BF16)

    for_chunks(rows // chunk, transition)

    side = jnp.concatenate([ln_scr[i * seqs : (i + 1) * seqs, :] for i in range(n_res)], axis=1)
    factors = dot(side, fg_ref[...])
    send_ref[0:seqs, :] = factors[:, :LANES].astype(BF16)
    for t in range(seqs // LANES):
        turned = factors[t * LANES : (t + 1) * LANES, LANES:].T.astype(BF16)
        if seqs & (seqs - 1) == 0:
            turned = (turned.astype(F32) * (1.0 / seqs)).astype(BF16)
        send_ref[seqs + t * LANES : seqs + (t + 1) * LANES, :] = turned
    by_row = lax.broadcasted_iota(jnp.int32, (16, LANES), 0)
    pairs = jnp.where(
        by_row < n_res, dot(amino_ref[...], re_ref[...]), dot(amino_ref[...], ce_ref[...])
    )
    send_ref[2 * seqs :, :] = pairs.astype(BF16)


def attention(x, amino, weights, large, ready, n_res):
    rows, feature = x.shape
    seqs = rows // n_res
    return local_call(
        functools.partial(attention_kernel, n_res),
        out_shape=(
            pltpu.VMEM((rows, feature), BF16),
            pltpu.VMEM((2 * seqs + 16, LANES), BF16),
        ),
        in_specs=[VMEM] * (2 + len(weights)) + [HBM] * (len(large) + len(ready)),
        out_specs=(VMEM, VMEM),
        scratch_shapes=[
            pltpu.VMEM((feature // LANES, rows, LANES), F32),
            pltpu.VMEM((rows, feature), F32),
            pltpu.VMEM((rows, feature), BF16),
            pltpu.VMEM((rows, feature), BF16),
            pltpu.VMEM((rows, feature), BF16),
            pltpu.VMEM((rows, feature), F32),
            pltpu.VMEM((rows, feature), BF16),
            pltpu.VMEM((rows, feature), BF16),
            *[pltpu.VMEM(w.shape, BF16) for w in large],
            pltpu.SemaphoreType.DMA((len(large),)),
        ],
        name="attention",
    )(near(x), near(amino), *[near(w) for w in weights], *[far(w) for w in (*large, *ready)])


def placement(n_row, n_col, places):
    my_row = lax.axis_index("row")
    my_col = lax.axis_index("col")
    half = n_row // 2
    row_place = [my_col ^ (2 * (slot % half) + slot // half) for slot in range(n_row)]
    line = []
    for offset in range(n_col):
        entry = jnp.int32(places[offset])
        for column in range(1, n_row):
            entry = jnp.where(my_col == column, places[column * n_col + offset], entry)
        line.append(entry)
    source_row = my_col // (n_row // n_col)
    col_place = []
    for slot in range(n_col):
        key = my_row ^ slot ^ source_row
        where = line[0]
        for offset in range(1, n_col):
            where = jnp.where(key == offset, line[offset], where)
        col_place.append(where)
    return my_row, my_col, row_place, col_place


def relative_kernel(n_row, n_col, n_res, places, off_ref, o_ref, swap_ref, off_scr):
    my_row, my_col, row_place, col_place = placement(n_row, n_col, places)
    count_i, count_j = n_row * n_res, n_col * n_res
    row_start = my_row * count_i
    col_start = my_col * count_j
    bins = lax.broadcasted_iota(jnp.int32, (count_j, LANES), 1)
    j_here = col_start + lax.broadcasted_iota(jnp.int32, (count_j, LANES), 0)
    bins_m = lax.broadcasted_iota(jnp.int32, (count_i, LANES), 1)
    i_slot = lax.broadcasted_iota(jnp.int32, (count_i, LANES), 0)
    i_here = i_slot % n_res + row_start
    for slot in range(n_row):
        i_here = jnp.where(i_slot // n_res == slot, i_here + row_place[slot] * n_res, i_here)

    def relative(offset, lanes):
        index = jnp.clip(offset, -CLIP, CLIP) + CLIP
        return jnp.where(index == lanes, 1.0, 0.0).astype(BF16)

    marks = []
    for slot in range(n_row):
        for r in range(n_res):
            i = row_start + row_place[slot] * n_res + r
            marks.append(relative(j_here - i, bins))
    for slot in range(n_col):
        for r in range(n_res):
            j = col_start + col_place[slot] * n_res + r
            marks.append(relative(i_here - j, bins_m))
    off_scr[...] = jnp.zeros_like(off_scr)
    off_scr[0 : off_ref.shape[0], :] = off_ref[...].astype(F32)
    o_ref[...] = dot(jnp.concatenate(marks, axis=0), off_scr[...].astype(BF16)).astype(BF16)

    width = swap_ref.shape[1]
    chunk = min(swap_ref.shape[0], 128)
    source = lax.broadcasted_iota(jnp.int32, (chunk, width), 1)
    slot_of = source // (n_res * count_i)
    place = jnp.zeros_like(source)
    for slot in range(n_col):
        place = jnp.where(slot_of == slot, col_place[slot], place)
    goal = (source % count_i) * count_j + place * n_res + source // count_i % n_res
    line = lax.broadcasted_iota(jnp.int32, (chunk, width), 0)
    for start in range(0, swap_ref.shape[0], chunk):
        swap_ref[start : start + chunk, :] = jnp.where(goal == line + start, 1.0, 0.0).astype(BF16)


def relative_rows(places, table, n_row, n_col, n_res):
    cells = n_row * n_col * n_res * n_res
    swapped = cells if cells <= SWAP_LIMIT else LANES
    return local_call(
        functools.partial(relative_kernel, n_row, n_col, n_res, places),
        out_shape=(pltpu.HBM((2 * cells, LANES), BF16), pltpu.HBM((swapped, swapped), BF16)),
        in_specs=[VMEM],
        out_specs=(VMEM, VMEM),
        scratch_shapes=[pltpu.VMEM((LANES, LANES), F32)],
        name="relative",
    )(near(table))


def pair_kernel(n_row, n_col, n_res, seqs, places, *refs):
    row_refs = refs[0:n_row]
    col_refs = refs[n_row : n_row + n_col]
    refs = refs[n_row + n_col :]
    rel_ref, swap_ref, bins_ref, wp_far, w1_far, w2_far, pair_far, dist_far = refs[:8]
    (a_r, a_c, lhs, grid, logit_scr) = refs[8:13]
    wp_ref, w1_ref, w2_ref, bd_ref, pair_ref, dist_ref, arrived, left_sem = refs[13:]
    fetches = [
        pltpu.make_async_copy(away, local, arrived.at[k])
        for k, (away, local) in enumerate(((wp_far, wp_ref), (w1_far, w1_ref), (w2_far, w2_ref)))
    ]
    for fetch in fetches:
        fetch.start()
    factor = LANES // n_res
    count_i = n_row * n_res
    count_j = n_col * n_res
    _, _, row_place, col_place = placement(n_row, n_col, places)

    def clear(e):
        for r in range(n_res):
            row = (e * n_res + r) * factor
            for other in range(n_res):
                if other != r:
                    bd_ref[row : row + factor, other * LANES : (other + 1) * LANES] = jnp.zeros(
                        (factor, LANES), BF16
                    )

    def fill(e):
        block = wp_ref[e * factor : (e + 1) * factor, :]
        for r in range(n_res):
            row = (e * n_res + r) * factor
            bd_ref[row : row + factor, r * LANES : (r + 1) * LANES] = block

    def gather_rows(count, places):
        width = GROUP * count
        line = lax.broadcasted_iota(jnp.int32, (width, width), 0)
        column = lax.broadcasted_iota(jnp.int32, (width, width), 1)
        piece = column // (GROUP * n_res)
        place = piece
        if places is not None:
            for slot, where in enumerate(places):
                place = jnp.where(piece == slot, where, place)
        goal = column % GROUP * count + place * n_res + column // GROUP % n_res
        return jnp.where(line == goal, 1.0, 0.0).astype(BF16)

    def stack(pieces, g):
        lanes = []
        for t in range(seqs // LANES):
            first = seqs + t * LANES + g * GROUP * n_res
            lanes.append(
                jnp.concatenate([p[first : first + GROUP * n_res, :] for p in pieces], axis=0)
            )
        return jnp.concatenate(lanes, axis=1)

    gather_c = gather_rows(count_j, col_place)
    gather_r = gather_rows(count_i, None)
    groups = factor // GROUP
    for g in range(groups):
        a_c[g * GROUP * count_j : (g + 1) * GROUP * count_j, :] = dot(
            gather_c, stack(col_refs, g)
        ).astype(BF16)
        a_r[g * GROUP * count_i : (g + 1) * GROUP * count_i, :] = dot(
            gather_r, stack(row_refs, g)
        ).astype(BF16)
        for e in range(g * GROUP, (g + 1) * GROUP):
            clear(e)
    for fetch in fetches:
        fetch.wait()
    todo = list(range(factor))

    exact = seqs & (seqs - 1) == 0

    def outer(a_ref, count, pieces, base):
        rows = factor * count
        chunk = min(rows, 1024)
        per = chunk // count
        step_pieces = 2
        for s in range(0, len(pieces), step_pieces):
            left = jnp.concatenate([p[0:seqs, :] for p in pieces[s : s + step_pieces]], axis=1)

            def one(step):
                made = dot(a_ref[rows_at(step * chunk, chunk), :], left)
                if not exact:
                    made = made * (1.0 / seqs)
                made = made.astype(BF16)
                for k in range(step_pieces):
                    for e in range(per):
                        lane = (step * per + e) * LANES
                        if not isinstance(lane, int):
                            lane = pl.multiple_of(lane, LANES)
                        lhs[
                            base + (s + k) * count : base + (s + k + 1) * count, pl.ds(lane, LANES)
                        ] = made[e * count : (e + 1) * count, k * LANES : (k + 1) * LANES]

            for_chunks(rows // chunk, one)
            for _ in range(min(share, len(todo))):
                fill(todo.pop())

    share = -(-factor * 2 // (n_row + n_col))
    direct = n_row * count_j
    mirrored = n_col * count_i
    outer(a_c, count_j, row_refs, 0)
    outer(a_r, count_i, col_refs, direct)

    while todo:
        fill(todo.pop())

    row_side = jnp.concatenate([r[2 * seqs : 2 * seqs + 16, :] for r in row_refs], axis=0)
    col_side = jnp.concatenate([r[2 * seqs : 2 * seqs + 16, :] for r in col_refs], axis=0)

    def pick(side, places, count):
        width = side.shape[0]
        line = lax.broadcasted_iota(jnp.int32, (count, width), 0)
        column = lax.broadcasted_iota(jnp.int32, (count, width), 1)
        goal = column % 16 - n_res
        place = jnp.zeros_like(column)
        for slot, where in enumerate(places):
            place = jnp.where(column // 16 == slot, where, place)
        hit = (goal >= 0) & (goal < n_res) & (line == place * n_res + goal)
        return dot(jnp.where(hit, 1.0, 0.0).astype(BF16), side)

    right_r = pick(row_side, list(range(n_row)), count_i)
    right_c = pick(col_side, col_place, count_j)
    total = direct + mirrored
    chunk = min(total, 256)

    def project(step):
        at = rows_at(step * chunk, chunk)
        made = dot(lhs[at, :], bd_ref[...])
        lhs_out[at, :] = made

    lhs_out = grid[1]
    start = grid[0]
    for_chunks(total // chunk, project)
    side_r = row_side.astype(F32)
    side_c = col_side.astype(F32)
    place = 0
    for slot in range(n_row):
        for r in range(n_res):
            made = lhs_out[slot * count_j : (slot + 1) * count_j, r * LANES : (r + 1) * LANES]
            left = side_r[slot * 16 + r : slot * 16 + r + 1, :]
            start[place : place + count_j, :] = (
                (left + right_c) + rel_ref[place : place + count_j, :] + made
            )
            place += count_j
    for slot in range(n_col):
        for r in range(n_res):
            made = lhs_out[
                direct + slot * count_i : direct + (slot + 1) * count_i,
                r * LANES : (r + 1) * LANES,
            ]
            left = side_c[slot * 16 + r : slot * 16 + r + 1, :]
            start[place : place + count_i, :] = (
                (left + right_r) + rel_ref[place : place + count_i, :] + made
            )
            place += count_i

    cells = count_i * count_j
    n_bins = dist_ref.shape[2]
    chunk2 = min(cells, 512)
    rounded_scr, all_logits = grid[2], grid[3]

    def transition(step):
        at = rows_at(step * chunk2, chunk2)
        begin = start[at, :]
        hidden = jnp.maximum(dot(standardize(begin).astype(BF16), w1_ref[...]), 0.0).astype(BF16)
        final = (begin + dot(hidden, w2_ref[...])).astype(BF16)
        rounded_scr[at, :] = final
        if swap_ref.shape[0] == cells:
            return
        all_logits[at, :] = lax.dot_general(
            final, bins_ref[...], (((1,), (1,)), ((), ())), preferred_element_type=F32
        )

    steps = cells // chunk2
    for_chunks(steps, transition)
    for slot in range(n_row):
        for r in range(n_res):
            at = (slot * n_res + r) * count_j
            goal = row_place[slot] * n_res + r
            pair_ref[goal] = rounded_scr[at : at + count_j, :]
    leave_pair = pltpu.make_async_copy(pair_ref, pair_far, left_sem.at[0])
    leave_pair.start()
    if steps == 1:
        transition(1)
    else:
        for_chunks(steps, lambda step: transition(step + steps))
    if swap_ref.shape[0] == cells:
        swapped = dot(swap_ref[...], rounded_scr[cells:, :]).astype(BF16)
        both = jnp.concatenate([rounded_scr[:cells, :], swapped], axis=1)
        twice = jnp.concatenate([bins_ref[...], bins_ref[...]], axis=1)
        made = lax.dot_general(
            both, twice, (((1,), (1,)), ((), ())), preferred_element_type=F32
        ).astype(BF16)
        leaves = [leave_pair]
        for slot in range(n_row):
            for r in range(n_res):
                at = (slot * n_res + r) * count_j
                dist_ref[row_place[slot] * n_res + r] = made[at : at + count_j, :]
        leave = pltpu.make_async_copy(dist_ref, dist_far, left_sem.at[1])
        leave.start()
        leave_pair.wait()
        leave.wait()
        return
    for slot in range(n_col):
        for r in range(n_res):
            source = cells + (slot * n_res + r) * count_i
            goal = (col_place[slot] * n_res + r) * count_i
            logit_scr[rows_at(goal, count_i), :n_bins] = all_logits[source : source + count_i, :]
    leaves = [leave_pair]
    for slot in range(n_row):
        for r in range(n_res):
            at = (slot * n_res + r) * count_j
            goal = row_place[slot] * n_res + r
            mirror = logit_scr[pl.ds(slot * n_res + r, count_j, stride=count_i), :]
            summed = all_logits[at : at + count_j, :] + mirror[:, :n_bins]
            dist_ref[goal] = summed.astype(BF16)
        rows = pl.ds(row_place[slot] * n_res, n_res)
        leave = pltpu.make_async_copy(dist_ref.at[rows], dist_far.at[rows], left_sem.at[1 + slot])
        leave.start()
        leaves.append(leave)
    for leave in leaves:
        leave.wait()


def pair_grid(places, row_pieces, col_pieces, weights, large, n_res, seqs):
    n_row, n_col = len(row_pieces), len(col_pieces)
    count_i, count_j = n_row * n_res, n_col * n_res
    factor = LANES // n_res
    total = n_row * count_j + n_col * count_i
    cells = count_i * count_j
    n_bins = weights[2].shape[0]
    return local_call(
        functools.partial(pair_kernel, n_row, n_col, n_res, seqs, places),
        out_shape=(
            jax.ShapeDtypeStruct((count_i, count_j, LANES), BF16),
            jax.ShapeDtypeStruct((count_i, count_j, n_bins), BF16),
        ),
        in_specs=[VMEM] * (n_row + n_col + len(weights)) + [HBM] * len(large),
        out_specs=(HBM, HBM),
        scratch_shapes=[
            pltpu.VMEM((factor * count_i, seqs), BF16),
            pltpu.VMEM((factor * count_j, seqs), BF16),
            pltpu.VMEM((total, factor * LANES), BF16),
            (
                pltpu.VMEM((2 * cells, LANES), F32),
                pltpu.VMEM((total, n_res * LANES), F32),
                pltpu.VMEM((2 * cells, LANES), BF16),
                pltpu.VMEM((2 * cells, n_bins), F32),
            ),
            pltpu.VMEM((cells, LANES), F32),
            *[pltpu.VMEM(w.shape, BF16) for w in large],
            pltpu.VMEM((factor * LANES, n_res * LANES), BF16),
            pltpu.VMEM((count_i, count_j, LANES), BF16),
            pltpu.VMEM((count_i, count_j, n_bins), BF16),
            pltpu.SemaphoreType.DMA((len(large),)),
            pltpu.SemaphoreType.DMA((1 + n_row,)),
        ],
        name="pairs",
    )(*[near(v) for v in (*row_pieces, *col_pieces, *weights)], *[far(w) for w in large])


def plane_offsets(n_row, n_col):
    offsets = []
    by_hops = sorted(range(n_row), key=lambda v: (bin(v).count("1"), v))
    for column in range(n_col):
        home = column // 2
        far = sorted(
            range(n_row),
            key=lambda m: (-abs((column * n_row + m) % n_col // 2 - home), m),
        )
        line = [0] * n_row
        for position, m in enumerate(far):
            line[m] = by_hops[position]
        offsets.append(line)
    return offsets


def shards(
    n_rows,
    n_cols,
    homolog_stack,
    per_amino_features,
    asking_matrix,
    lookup_matrix,
    content_matrix,
    sigmoid_scaling_matrix,
    attention_result_matrix,
    stack_transition_expand_matrix,
    stack_transition_shrink_matrix,
    former_factor_matrix,
    latter_factor_matrix,
    factor_mean_projection,
    row_amino_embedding,
    column_amino_embedding,
    offset_embedding_matrix,
    grid_transition_expand,
    grid_transition_shrink,
    distance_bins_matrix,
):
    devices = n_rows * n_cols
    n_seq, amino, feature = homolog_stack.shape
    n_res = amino // devices
    seqs = n_seq * devices
    axes = ("row", "col")

    sent = chunks(homolog_stack, n_res).reshape(devices, n_seq * n_res, feature)
    moved = lax.all_to_all(sent, axes, split_axis=0, concat_axis=0, tiled=True)
    moved = moved.reshape(seqs * n_res, feature)

    unit = jnp.eye(n_res, dtype=BF16)
    grouped = latter_factor_matrix.reshape(feature, -1, GROUP)
    latter = jnp.einsum("pr,fge->pfgre", unit, grouped).reshape(n_res * feature, -1)
    factors = jnp.concatenate([jnp.kron(unit, former_factor_matrix), latter], axis=1)
    amino_rows = jnp.concatenate(
        [per_amino_features, per_amino_features, jnp.zeros((16 - 2 * n_res, feature), BF16)], axis=0
    )
    projection = turn_projection(factor_mean_projection)
    table = plane_offsets(n_rows, n_cols)
    inverse = []
    for line in table:
        back = [0] * n_rows
        for m, offset in enumerate(line):
            back[offset] = m
        inverse.extend(back)
    relative, swap = relative_rows(inverse, offset_embedding_matrix, n_cols, n_rows, n_res)

    aligned, piece = attention(
        moved,
        amino_rows,
        (
            asking_matrix,
            lookup_matrix,
            content_matrix,
            sigmoid_scaling_matrix,
            attention_result_matrix,
            factors,
            row_amino_embedding,
            column_amino_embedding,
        ),
        (stack_transition_expand_matrix, stack_transition_shrink_matrix),
        (projection, relative),
        n_res,
    )
    alignment_output = aligned.reshape(n_res, seqs, feature).transpose(1, 0, 2)

    turn = []
    for p in range(devices):
        column, m = p // n_rows, p % n_rows
        turn.append((p, ((p // n_cols) ^ table[column][m]) * n_cols + column))
    turned = lax.ppermute(piece, axes, turn)

    def along_col(value, m):
        return lax.ppermute(value, "col", [(c, c ^ m) for c in range(n_cols)])

    def along_row(value, m):
        return lax.ppermute(value, "row", [(r, r ^ m) for r in range(n_rows)])

    own = [piece] + [along_col(piece, 2 * m) for m in range(1, n_cols // 2)]
    other = [along_col(value, 1) for value in own]
    col_pieces = [turned] + [along_row(turned, m) for m in range(1, n_rows)]

    pair_output, distogram = pair_grid(
        inverse,
        own + other,
        col_pieces,
        (
            relative,
            swap,
            distance_bins_matrix.T,
        ),
        (projection, grid_transition_expand, grid_transition_shrink),
        n_res,
        seqs,
    )
    return (alignment_output, pair_output, distogram)


def solution(mesh):
    n_rows, n_cols = mesh.shape["row"], mesh.shape["col"]
    assert n_cols == 2 * n_rows and n_rows & (n_rows - 1) == 0
    placed = (P(("row", "col"), None, None), P(("row", "col"), None)) + (P(),) * 16
    return jax.shard_map(
        functools.partial(shards, n_rows, n_cols),
        mesh=mesh,
        in_specs=placed,
        out_specs=(P(None, ("row", "col"), None), P("row", "col", None), P("row", "col", None)),
        check_vma=False,
    )
```

profile of v0, /device:TPU:0, one launch (start us, length us, event | category | flops | bytes accessed | tf_op | source)
XLA Modules:
  0.0 43.9 jit_solution(7456546576402466689)
XLA Ops:
  0.6 1.7 %chunks.1 = bf16[512,256]{1,0:T(8,128)(2,1)} custom-call(bf16[4,128,256]{2,1,0:T(8,128)(2,1)} %x_far.1), custom_call_target="tpu_custom_call" | custom-call | tf_op jit(solution)/shard_map/chunks/pallas_call | solution.py:107
  2.3 0.0 copy-start.13
  2.3 7.3 %all-to-all-start = ((bf16[32,16,256]{2,1,0:T(8,128)(2,1)}), bf16[32,16,256]{2,1,0:T(8,128)(2,1)S(1)}, u32[]{:S(2)}, u32[]{:S(2)}) async-start(bf16[32,16,256]{2,1,0:T(8,128)(2,1)} %bitcast.23), calls=%async_computation | async-start | bytes 524288 | tf_op jit(solution)/shard_map/all_to_all | solution.py:676
  9.7 0.2 broadcast_multiply_fusion
  9.9 0.2 copy.25
  10.1 0.5 %copy-done.12 = bf16[256,32]{0,1:T(8,128)(2,1)S(1)} copy-done((bf16[256,32]{0,1:T(8,128)(2,1)S(1)}, bf16[256,32]{0,1:T(8,128)(2,1)}, u32[]{:S(2)}) %copy-start.12) | copy-done | bytes 16408
  10.6 0.2 broadcast_multiply_fusion.1
  10.8 0.0 copy-start.2
  10.8 0.2 copy.24
  11.0 0.8 %copy-done.2 = bf16[1024,128]{1,0:T(8,128)(2,1)S(1)} copy-done((bf16[1024,128]{1,0:T(8,128)(2,1)S(1)}, bf16[1024,128]{1,0:T(8,128)(2,1)}, u32[]{:S(2)}) %copy-start.2) | copy-done | bytes 262168
  11.8 1.0 %turn.1._.refs_15_ = bf16[1024,128]{1,0:T(8,128)(2,1)} custom-call(bf16[1024,128]{1,0:T(8,128)(2,1)S(1)} %copy-done.2), custom_call_target="tpu_custom_call" | custom-call | tf_op jit(solution)/shard_map/turn/pallas_call | solution.py:132
  12.8 1.2 %relative.1 = (bf16[1024,128]{1,0:T(8,128)(2,1)}, bf16[512,512]{1,0:T(8,128)(2,1)}) custom-call(bf16[65,128]{1,0:T(8,128)(2,1)S(1)} %copy-done.10), custom_call_target="tpu_custom_call" | custom-call | tf_op jit(solution)/shard_map/relative/pallas_call | solution.py:359
  14.1 0.1 pad.4.clone
  14.2 0.0 copy-start.7
  14.2 0.0 copy-start.8
  14.2 0.1 pad_maximum_fusion.fg_ref
  14.3 0.6 %copy-done.14 = bf16[4,256]{1,0:T(4,128)(2,1)S(1)} copy-done((bf16[4,256]{1,0:T(4,128)(2,1)S(1)}, bf16[4,256]{1,0:T(4,128)(2,1)}, u32[]{:S(2)}) %copy-start.14) | copy-done | bytes 2072
  14.8 0.1 maximum_maximum_fusion.amino_ref
  14.9 4.7 %all-to-all-done = bf16[32,16,256]{2,1,0:T(8,128)(2,1)S(1)} async-done(((bf16[32,16,256]{2,1,0:T(8,128)(2,1)}), bf16[32,16,256]{2,1,0:T(8,128)(2,1)S(1)}, u32[]{:S(2)}, u32[]{:S(2)}) %all-to-all-start) | async-done | bytes 262176 | tf_op jit(solution)/shard_map/all_to_all | solution.py:676
  19.7 3.3 %attention.1 = (bf16[512,256]{1,0:T(8,128)(2,1)S(1)}, bf16[272,128]{1,0:T(8,128)(2,1)S(1)}) custom-call(bf16[512,256]{1,0:T(8,128)(2,1)S(1)} %bitcast.20, bf16[16,256]{1,0:T(8,128)(2,1)S(1)} %maximum_maximum_fusion.amino_ref, bf16[256,256]{1,0:T(8,128)(2,1)S(1)} %copy-done.3, bf16[256,256]{1,0:T(8,128)(2,1)S(1)} %copy-done.4, ...), custom_call_target="tpu_custom_call" | custom-call | tf_op jit(solution)/shard_map/attention/pallas_call | solution.py:267
  23.0 0.9 %collective-permute-start.7 = (bf16[272,128]{1,0:T(8,128)(2,1)S(1)}, bf16[272,128]{1,0:T(8,128)(2,1)S(1)}, u32[]{:S(2)}, u32[]{:S(2)}) collective-permute-start(bf16[272,128]{1,0:T(8,128)(2,1)S(1)} %get-tuple-element.11.refs_0_), channel_id=1, source_target_pairs={{0,16},{1,24},{2,0},{3,8},{4,17},{5,25},{6,1},{7,9},{8,10},{9,2},{... | collective-permute-start | bytes 208904 | tf_op jit(solution)/shard_map/ppermute | solution.py:719
  24.0 0.4 collective-permute-start.3
  24.3 3.3 %collective-permute-start.2 = (bf16[272,128]{1,0:T(8,128)(2,1)S(1)}, bf16[272,128]{1,0:T(8,128)(2,1)S(1)}, u32[]{:S(2)}, u32[]{:S(2)}) collective-permute-start(bf16[272,128]{1,0:T(8,128)(2,1)S(1)} %get-tuple-element.11.refs_0_), channel_id=1, source_target_pairs={{0,6},{1,7},{2,4},{3,5},{4,2},{5,3},{6,0},{7,1},{8,14},{9,15},{10,... | collective-permute-start | bytes 208904 | tf_op jit(solution)/shard_map/ppermute | solution.py:722
  27.6 1.1 %collective-permute-start = (bf16[272,128]{1,0:T(8,128)(2,1)S(1)}, bf16[272,128]{1,0:T(8,128)(2,1)S(1)}, u32[]{:S(2)}, u32[]{:S(2)}) collective-permute-start(bf16[272,128]{1,0:T(8,128)(2,1)S(1)} %get-tuple-element.11.refs_0_), channel_id=1, source_target_pairs={{0,2},{1,3},{2,0},{3,1},{4,6},{5,7},{6,4},{7,5},{8,10},{9,11},{10,... | collective-permute-start | bytes 208904 | tf_op jit(solution)/shard_map/ppermute | solution.py:722
  28.7 3.3 %collective-permute-done.7.refs_8_ = bf16[272,128]{1,0:T(8,128)(2,1)S(1)} collective-permute-done((bf16[272,128]{1,0:T(8,128)(2,1)S(1)}, bf16[272,128]{1,0:T(8,128)(2,1)S(1)}, u32[]{:S(2)}, u32[]{:S(2)}) %collective-permute-start.7) | collective-permute-done | bytes 69664 | tf_op jit(solution)/shard_map/ppermute | solution.py:719
  32.0 3.5 %collective-permute-start.8 = (bf16[272,128]{1,0:T(8,128)(2,1)S(1)}, bf16[272,128]{1,0:T(8,128)(2,1)S(1)}, u32[]{:S(2)}, u32[]{:S(2)}) collective-permute-start(bf16[272,128]{1,0:T(8,128)(2,1)S(1)} %collective-permute-done.7.refs_8_), channel_id=1, source_target_pairs={{0,8},{8,0},{16,24},{24,16},{1,9},{9,1},{17,25},{25,17},{2,10},{10... | collective-permute-start | bytes 208904 | tf_op jit(solution)/shard_map/ppermute | solution.py:725
  35.5 1.0 %collective-permute-done.1.refs_2_ = bf16[272,128]{1,0:T(8,128)(2,1)S(1)} collective-permute-done((bf16[272,128]{1,0:T(8,128)(2,1)S(1)}, bf16[272,128]{1,0:T(8,128)(2,1)S(1)}, u32[]{:S(2)}, u32[]{:S(2)}) %collective-permute-start.1) | collective-permute-done | bytes 69664 | tf_op jit(solution)/shard_map/ppermute | solution.py:722
  36.5 0.5 %collective-permute-start.5 = (bf16[272,128]{1,0:T(8,128)(2,1)S(1)}, bf16[272,128]{1,0:T(8,128)(2,1)S(1)}, u32[]{:S(2)}, u32[]{:S(2)}) collective-permute-start(bf16[272,128]{1,0:T(8,128)(2,1)S(1)} %collective-permute-done.1.refs_2_), channel_id=1, source_target_pairs={{0,1},{1,0},{2,3},{3,2},{4,5},{5,4},{6,7},{7,6},{8,9},{9,8},{10,11... | collective-permute-start | bytes 208904 | tf_op jit(solution)/shard_map/ppermute | solution.py:722
  37.0 0.3 collective-permute-done.10.refs_11_
  37.3 0.9 %copy.30 = bf16[4,128,256]{2,0,1:T(4,128)(2,1)} copy(bf16[4,128,256]{2,1,0:T(8,128)(2,1)S(1)} %bitcast.21) | data formatting | bytes 524288 | tf_op jit(solution)/shard_map/reshape | solution.py:713
  38.3 0.3 collective-permute-done.4.refs_5_
  38.6 5.3 %pairs.1 = (bf16[32,16,128]{2,1,0:T(8,128)(2,1)}, bf16[32,16,64]{2,1,0:T(8,128)(2,1)}) custom-call(bf16[272,128]{1,0:T(8,128)(2,1)S(1)} %get-tuple-element.11.refs_0_, bf16[272,128]{1,0:T(8,128)(2,1)S(1)} %collective-permute-done.refs_1_, bf16[272,128]{1,0:T(8,128)(2,1)S(1)} %collective-permute-done.1.refs_2_, ...), custom_call_target="tpu_custom_call" | custom-call | tf_op jit(solution)/shard_map/pairs/pallas_call | solution.py:601
  (40 shorter events, 0.2 us)
Async XLA Ops:
  2.3 7.4 %copy-start.13 = (bf16[256,32]{0,1:T(8,128)(2,1)S(1)}, bf16[256,32]{0,1:T(8,128)(2,1)}, u32[]{:S(2)}) copy-start(bf16[256,32]{0,1:T(8,128)(2,1)} %param.28) | copy-start | bytes 49156
  2.3 17.3 %all-to-all-start = ((bf16[32,16,256]{2,1,0:T(8,128)(2,1)}), bf16[32,16,256]{2,1,0:T(8,128)(2,1)S(1)}, u32[]{:S(2)}, u32[]{:S(2)}) async-start(bf16[32,16,256]{2,1,0:T(8,128)(2,1)} %bitcast.23), calls=%async_computation | async-start | bytes 524288 | tf_op jit(solution)/shard_map/all_to_all | solution.py:676
  9.9 0.7 %copy-start.12 = (bf16[256,32]{0,1:T(8,128)(2,1)S(1)}, bf16[256,32]{0,1:T(8,128)(2,1)}, u32[]{:S(2)}) copy-start(bf16[256,32]{0,1:T(8,128)(2,1)} %param.27) | copy-start | bytes 49156
  10.8 1.0 %copy-start.2 = (bf16[1024,128]{1,0:T(8,128)(2,1)S(1)}, bf16[1024,128]{1,0:T(8,128)(2,1)}, u32[]{:S(2)}) copy-start(bf16[1024,128]{1,0:T(8,128)(2,1)} %w_ref.1) | copy-start | bytes 786436
  11.8 1.1 %copy-start.10 = (bf16[65,128]{1,0:T(8,128)(2,1)S(1)}, bf16[65,128]{1,0:T(8,128)(2,1)}, u32[]{:S(2)}) copy-start(bf16[65,128]{1,0:T(8,128)(2,1)} %off_ref.1) | copy-start | bytes 49924
  14.2 0.7 %copy-start.14 = (bf16[4,256]{1,0:T(4,128)(2,1)S(1)}, bf16[4,256]{1,0:T(4,128)(2,1)}, u32[]{:S(2)}) copy-start(bf16[4,256]{1,0:T(4,128)(2,1)} %param.19) | copy-start | bytes 6148
  14.2 5.5 %copy-start.3 = (bf16[256,256]{1,0:T(8,128)(2,1)S(1)}, bf16[256,256]{1,0:T(8,128)(2,1)}, u32[]{:S(2)}) copy-start(bf16[256,256]{1,0:T(8,128)(2,1)} %wq_ref.1) | copy-start | bytes 393220
  14.2 5.5 %copy-start.4 = (bf16[256,256]{1,0:T(8,128)(2,1)S(1)}, bf16[256,256]{1,0:T(8,128)(2,1)}, u32[]{:S(2)}) copy-start(bf16[256,256]{1,0:T(8,128)(2,1)} %wk_ref.1) | copy-start | bytes 393220
  14.2 5.5 %copy-start.5 = (bf16[256,256]{1,0:T(8,128)(2,1)S(1)}, bf16[256,256]{1,0:T(8,128)(2,1)}, u32[]{:S(2)}) copy-start(bf16[256,256]{1,0:T(8,128)(2,1)} %wv_ref.1) | copy-start | bytes 393220
  14.2 5.5 %copy-start.6 = (bf16[256,256]{1,0:T(8,128)(2,1)S(1)}, bf16[256,256]{1,0:T(8,128)(2,1)}, u32[]{:S(2)}) copy-start(bf16[256,256]{1,0:T(8,128)(2,1)} %wg_ref.1) | copy-start | bytes 393220
  14.2 5.5 %copy-start.7 = (bf16[256,256]{1,0:T(8,128)(2,1)S(1)}, bf16[256,256]{1,0:T(8,128)(2,1)}, u32[]{:S(2)}) copy-start(bf16[256,256]{1,0:T(8,128)(2,1)} %wo_ref.1) | copy-start | bytes 393220
  14.2 5.5 %copy-start.8 = (bf16[256,128]{1,0:T(8,128)(2,1)S(1)}, bf16[256,128]{1,0:T(8,128)(2,1)}, u32[]{:S(2)}) copy-start(bf16[256,128]{1,0:T(8,128)(2,1)} %re_ref.1) | copy-start | bytes 196612
  14.2 5.5 %copy-start.9 = (bf16[256,128]{1,0:T(8,128)(2,1)S(1)}, bf16[256,128]{1,0:T(8,128)(2,1)}, u32[]{:S(2)}) copy-start(bf16[256,128]{1,0:T(8,128)(2,1)} %ce_ref.1) | copy-start | bytes 196612
  19.7 18.9 %copy-start.1 = (bf16[512,512]{1,0:T(8,128)(2,1)S(1)}, bf16[512,512]{1,0:T(8,128)(2,1)}, u32[]{:S(2)}) copy-start(bf16[512,512]{1,0:T(8,128)(2,1)} %get-tuple-element.12.refs_13_) | copy-start | bytes 1572868
  23.0 9.0 %collective-permute-start.7 = (bf16[272,128]{1,0:T(8,128)(2,1)S(1)}, bf16[272,128]{1,0:T(8,128)(2,1)S(1)}, u32[]{:S(2)}, u32[]{:S(2)}) collective-permute-start(bf16[272,128]{1,0:T(8,128)(2,1)S(1)} %get-tuple-element.11.refs_0_), channel_id=1, source_target_pairs={{0,16},{1,24},{2,0},{3,8},{4,17},{5,25},{6,1},{7,9},{8,10},{9,2},{... | collective-permute-start | bytes 208904 | tf_op jit(solution)/shard_map/ppermute | solution.py:719
  24.0 8.1 %collective-permute-start.3 = (bf16[272,128]{1,0:T(8,128)(2,1)S(1)}, bf16[272,128]{1,0:T(8,128)(2,1)S(1)}, u32[]{:S(2)}, u32[]{:S(2)}) collective-permute-start(bf16[272,128]{1,0:T(8,128)(2,1)S(1)} %get-tuple-element.11.refs_0_), channel_id=1, source_target_pairs={{0,1},{1,0},{2,3},{3,2},{4,5},{5,4},{6,7},{7,6},{8,9},{9,8},{10,11... | collective-permute-start | bytes 208904 | tf_op jit(solution)/shard_map/ppermute | solution.py:722
  24.3 7.7 %collective-permute-start.2 = (bf16[272,128]{1,0:T(8,128)(2,1)S(1)}, bf16[272,128]{1,0:T(8,128)(2,1)S(1)}, u32[]{:S(2)}, u32[]{:S(2)}) collective-permute-start(bf16[272,128]{1,0:T(8,128)(2,1)S(1)} %get-tuple-element.11.refs_0_), channel_id=1, source_target_pairs={{0,6},{1,7},{2,4},{3,5},{4,2},{5,3},{6,0},{7,1},{8,14},{9,15},{10,... | collective-permute-start | bytes 208904 | tf_op jit(solution)/shard_map/ppermute | solution.py:722
  27.6 8.9 %collective-permute-start.1 = (bf16[272,128]{1,0:T(8,128)(2,1)S(1)}, bf16[272,128]{1,0:T(8,128)(2,1)S(1)}, u32[]{:S(2)}, u32[]{:S(2)}) collective-permute-start(bf16[272,128]{1,0:T(8,128)(2,1)S(1)} %get-tuple-element.11.refs_0_), channel_id=1, source_target_pairs={{0,4},{1,5},{2,6},{3,7},{4,0},{5,1},{6,2},{7,3},{8,12},{9,13},{10,... | collective-permute-start | bytes 208904 | tf_op jit(solution)/shard_map/ppermute | solution.py:722
  27.6 8.9 %collective-permute-start = (bf16[272,128]{1,0:T(8,128)(2,1)S(1)}, bf16[272,128]{1,0:T(8,128)(2,1)S(1)}, u32[]{:S(2)}, u32[]{:S(2)}) collective-permute-start(bf16[272,128]{1,0:T(8,128)(2,1)S(1)} %get-tuple-element.11.refs_0_), channel_id=1, source_target_pairs={{0,2},{1,3},{2,0},{3,1},{4,6},{5,7},{6,4},{7,5},{8,10},{9,11},{10,... | collective-permute-start | bytes 208904 | tf_op jit(solution)/shard_map/ppermute | solution.py:722
  32.0 5.3 %collective-permute-start.10 = (bf16[272,128]{1,0:T(8,128)(2,1)S(1)}, bf16[272,128]{1,0:T(8,128)(2,1)S(1)}, u32[]{:S(2)}, u32[]{:S(2)}) collective-permute-start(bf16[272,128]{1,0:T(8,128)(2,1)S(1)} %collective-permute-done.7.refs_8_), channel_id=1, source_target_pairs={{0,24},{8,16},{16,8},{24,0},{1,25},{9,17},{17,9},{25,1},{2,26},{10... | collective-permute-start | bytes 208904 | tf_op jit(solution)/shard_map/ppermute | solution.py:725
  32.0 6.2 %collective-permute-start.9 = (bf16[272,128]{1,0:T(8,128)(2,1)S(1)}, bf16[272,128]{1,0:T(8,128)(2,1)S(1)}, u32[]{:S(2)}, u32[]{:S(2)}) collective-permute-start(bf16[272,128]{1,0:T(8,128)(2,1)S(1)} %collective-permute-done.7.refs_8_), channel_id=1, source_target_pairs={{0,16},{8,24},{16,0},{24,8},{1,17},{9,25},{17,1},{25,9},{2,18},{10... | collective-permute-start | bytes 208904 | tf_op jit(solution)/shard_map/ppermute | solution.py:725
  32.0 6.2 %collective-permute-start.8 = (bf16[272,128]{1,0:T(8,128)(2,1)S(1)}, bf16[272,128]{1,0:T(8,128)(2,1)S(1)}, u32[]{:S(2)}, u32[]{:S(2)}) collective-permute-start(bf16[272,128]{1,0:T(8,128)(2,1)S(1)} %collective-permute-done.7.refs_8_), channel_id=1, source_target_pairs={{0,8},{8,0},{16,24},{24,16},{1,9},{9,1},{17,25},{25,17},{2,10},{10... | collective-permute-start | bytes 208904 | tf_op jit(solution)/shard_map/ppermute | solution.py:725
  36.5 1.8 %collective-permute-start.6 = (bf16[272,128]{1,0:T(8,128)(2,1)S(1)}, bf16[272,128]{1,0:T(8,128)(2,1)S(1)}, u32[]{:S(2)}, u32[]{:S(2)}) collective-permute-start(bf16[272,128]{1,0:T(8,128)(2,1)S(1)} %collective-permute-done.2.refs_3_), channel_id=1, source_target_pairs={{0,1},{1,0},{2,3},{3,2},{4,5},{5,4},{6,7},{7,6},{8,9},{9,8},{10,11... | collective-permute-start | bytes 208904 | tf_op jit(solution)/shard_map/ppermute | solution.py:722
  36.5 1.8 %collective-permute-start.5 = (bf16[272,128]{1,0:T(8,128)(2,1)S(1)}, bf16[272,128]{1,0:T(8,128)(2,1)S(1)}, u32[]{:S(2)}, u32[]{:S(2)}) collective-permute-start(bf16[272,128]{1,0:T(8,128)(2,1)S(1)} %collective-permute-done.1.refs_2_), channel_id=1, source_target_pairs={{0,1},{1,0},{2,3},{3,2},{4,5},{5,4},{6,7},{7,6},{8,9},{9,8},{10,11... | collective-permute-start | bytes 208904 | tf_op jit(solution)/shard_map/ppermute | solution.py:722
  37.3 1.3 %collective-permute-start.4 = (bf16[272,128]{1,0:T(8,128)(2,1)S(1)}, bf16[272,128]{1,0:T(8,128)(2,1)S(1)}, u32[]{:S(2)}, u32[]{:S(2)}) collective-permute-start(bf16[272,128]{1,0:T(8,128)(2,1)S(1)} %collective-permute-done.refs_1_), channel_id=1, source_target_pairs={{0,1},{1,0},{2,3},{3,2},{4,5},{5,4},{6,7},{7,6},{8,9},{9,8},{10,11... | collective-permute-start | bytes 208904 | tf_op jit(solution)/shard_map/ppermute | solution.py:722
  37.3 1.3 %copy-start = (bf16[1024,128]{1,0:T(8,128)(2,1)S(1)}, bf16[1024,128]{1,0:T(8,128)(2,1)}, u32[]{:S(2)}) copy-start(bf16[1024,128]{1,0:T(8,128)(2,1)} %get-tuple-element.9._2.refs_12_) | copy-start | bytes 786436
  37.3 1.3 %copy-start.11 = (bf16[128,64]{0,1:T(8,128)(2,1)S(1)}, bf16[128,64]{0,1:T(8,128)(2,1)}, u32[]{:S(2)}) copy-start(bf16[128,64]{0,1:T(8,128)(2,1)} %param.35) | copy-start | bytes 49156
where the time goes:
time: 44.3 us; the launch traced here: 43.9 us
  starting transfers between devices  17 us (38%)
  Pallas kernels  12.5 us (28%)
  waiting for transfers between devices  9.66 us (22%)
  local copies, waits for them, and re-layouts  3.32 us (7%)
  between operations  0.87 us (2%)
  other arithmetic  0.47 us (1%)
    all_to_all x1, starting transfers between devices, shards(): moved = lax.all_to_all(sent, axes, split_axis=0, concat_axis=0, tiled=True)  7.33 us
    ppermute x7, starting transfers between devices, along_col(): return lax.ppermute(value, 'col', [(c, c ^ m) for c in range(n_cols)])  5.28 us
    pallas_call x1, Pallas kernels, pair_grid(): local_call(functools.partial(pair_kernel, n_row, n_col, n_res, seqs, plac...  5.27 us
    all_to_all x1, waiting for transfers between devices, shards(): moved = lax.all_to_all(sent, axes, split_axis=0, concat_axis=0, tiled=True)  4.73 us
    ppermute x3, starting transfers between devices, along_row(): return lax.ppermute(value, 'row', [(r, r ^ m) for r in range(n_rows)])  3.48 us
    pallas_call x1, Pallas kernels, attention(): local_call(functools.partial(attention_kernel, n_res), out_shape=(pltpu.V...  3.32 us
    ppermute x1, waiting for transfers between devices, shards(): turned = lax.ppermute(piece, axes, turn)  3.29 us
    unnamed x32, local copies, waits for them, and re-layouts  1.98 us
  transfers between devices with their start and end apart: 12, of which 5 were waited for; matrix products, arithmetic and copies ran while one was open for 4% of the time, Pallas kernels for 5%

commit v1 on v0

--- a/solution.py
+++ b/solution.py
@@ -12,6 +12,7 @@
 CLIP = 32
 LANES = 128
 GROUP = 4
+PAIR = 2
 SWAP_LIMIT = 512
 F32 = jnp.float32
 BF16 = jnp.bfloat16
@@ -151,8 +152,8 @@
     fg_ref,
     re_ref,
     ce_ref,
-    w1_far,
-    w2_far,
+    w1_ref,
+    w2_ref,
     _,
     _2,
     align_ref,
@@ -165,14 +166,7 @@
     g_scr,
     mix_scr,
     ln_scr,
-    w1_ref,
-    w2_ref,
-    arrived,
 ):
-    fetch_1 = pltpu.make_async_copy(w1_far, w1_ref, arrived.at[0])
-    fetch_2 = pltpu.make_async_copy(w2_far, w2_ref, arrived.at[1])
-    fetch_1.start()
-    fetch_2.start()
     rows, feature = x_ref.shape
     seqs = rows // n_res
     chunk = min(rows, 512)
@@ -233,9 +227,6 @@
 
         for_chunks(n_res, attend_all)
 
-    fetch_1.wait()
-    fetch_2.wait()
-
     def transition(step):
         at = rows_at(step * chunk, chunk)
         first = res_scr[at, :] + dot(mix_scr[at, :], wo_ref[...])
@@ -261,7 +252,7 @@
     send_ref[2 * seqs :, :] = pairs.astype(BF16)
 
 
-def attention(x, amino, weights, large, ready, n_res):
+def attention(x, amino, weights, ready, n_res):
     rows, feature = x.shape
     seqs = rows // n_res
     return local_call(
@@ -270,7 +261,7 @@
             pltpu.VMEM((rows, feature), BF16),
             pltpu.VMEM((2 * seqs + 16, LANES), BF16),
         ),
-        in_specs=[VMEM] * (2 + len(weights)) + [HBM] * (len(large) + len(ready)),
+        in_specs=[VMEM] * (2 + len(weights)) + [HBM] * len(ready),
         out_specs=(VMEM, VMEM),
         scratch_shapes=[
             pltpu.VMEM((feature // LANES, rows, LANES), F32),
@@ -281,11 +272,9 @@
             pltpu.VMEM((rows, feature), F32),
             pltpu.VMEM((rows, feature), BF16),
             pltpu.VMEM((rows, feature), BF16),
-            *[pltpu.VMEM(w.shape, BF16) for w in large],
-            pltpu.SemaphoreType.DMA((len(large),)),
         ],
         name="attention",
-    )(near(x), near(amino), *[near(w) for w in weights], *[far(w) for w in (*large, *ready)])
+    )(near(x), near(amino), *[near(w) for w in weights], *[far(w) for w in ready])
 
 
 def placement(n_row, n_col, places):
@@ -370,34 +359,24 @@
     row_refs = refs[0:n_row]
     col_refs = refs[n_row : n_row + n_col]
     refs = refs[n_row + n_col :]
-    rel_ref, swap_ref, bins_ref, wp_far, w1_far, w2_far, pair_far, dist_far = refs[:8]
+    rel_ref, swap_ref, bins_ref, wp_ref, w1_ref, w2_ref, pair_far, dist_far = refs[:8]
     (a_r, a_c, lhs, grid, logit_scr) = refs[8:13]
-    wp_ref, w1_ref, w2_ref, bd_ref, pair_ref, dist_ref, arrived, left_sem = refs[13:]
-    fetches = [
-        pltpu.make_async_copy(away, local, arrived.at[k])
-        for k, (away, local) in enumerate(((wp_far, wp_ref), (w1_far, w1_ref), (w2_far, w2_ref)))
-    ]
-    for fetch in fetches:
-        fetch.start()
+    bd_ref, pair_ref, dist_ref, left_sem = refs[13:]
     factor = LANES // n_res
     count_i = n_row * n_res
     count_j = n_col * n_res
     _, _, row_place, col_place = placement(n_row, n_col, places)
 
-    def clear(e):
-        for r in range(n_res):
-            row = (e * n_res + r) * factor
-            for other in range(n_res):
-                if other != r:
-                    bd_ref[row : row + factor, other * LANES : (other + 1) * LANES] = jnp.zeros(
-                        (factor, LANES), BF16
-                    )
+    halves = n_res // PAIR
 
     def fill(e):
         block = wp_ref[e * factor : (e + 1) * factor, :]
-        for r in range(n_res):
-            row = (e * n_res + r) * factor
-            bd_ref[row : row + factor, r * LANES : (r + 1) * LANES] = block
+        for r in range(PAIR):
+            row = (e * PAIR + r) * factor
+            for other in range(PAIR):
+                bd_ref[row : row + factor, other * LANES : (other + 1) * LANES] = (
+                    block if other == r else jnp.zeros_like(block)
+                )
 
     def gather_rows(count, places):
         width = GROUP * count
@@ -424,52 +403,63 @@
     gather_r = gather_rows(count_i, None)
     groups = factor // GROUP
     for g in range(groups):
-        a_c[g * GROUP * count_j : (g + 1) * GROUP * count_j, :] = dot(
-            gather_c, stack(col_refs, g)
-        ).astype(BF16)
-        a_r[g * GROUP * count_i : (g + 1) * GROUP * count_i, :] = dot(
-            gather_r, stack(row_refs, g)
-        ).astype(BF16)
-        for e in range(g * GROUP, (g + 1) * GROUP):
-            clear(e)
-    for fetch in fetches:
-        fetch.wait()
+        for a_ref, gather, pieces, count in (
+            (a_c, gather_c, col_refs, count_j),
+            (a_r, gather_r, row_refs, count_i),
+        ):
+            made = dot(gather, stack(pieces, g)).astype(BF16)
+            for k in range(GROUP):
+                row = (g * GROUP + k) // PAIR * count
+                lane = k % PAIR * seqs
+                a_ref[row : row + count, lane : lane + seqs] = made[k * count : (k + 1) * count, :]
     todo = list(range(factor))
 
     exact = seqs & (seqs - 1) == 0
+    width = LANES // PAIR
+    lane_half = lax.broadcasted_iota(jnp.int32, (seqs, LANES), 1) // width
+
+    def aside(value):
+        value = value.astype(F32)
+        rows = []
+        for e in range(PAIR):
+            tiles = []
+            for half in range(halves):
+                shifted = value if half == e else pltpu.roll(value, width, 1)
+                tiles.append(jnp.where(lane_half == e, shifted, 0.0))
+            rows.append(jnp.concatenate(tiles, axis=1))
+        return jnp.concatenate(rows, axis=0).astype(BF16)
 
     def outer(a_ref, count, pieces, base):
-        rows = factor * count
+        rows = factor // PAIR * count
         chunk = min(rows, 1024)
         per = chunk // count
-        step_pieces = 2
-        for s in range(0, len(pieces), step_pieces):
-            left = jnp.concatenate([p[0:seqs, :] for p in pieces[s : s + step_pieces]], axis=1)
+        for s, piece in enumerate(pieces):
+            left = aside(piece[0:seqs, :])
 
             def one(step):
                 made = dot(a_ref[rows_at(step * chunk, chunk), :], left)
                 if not exact:
                     made = made * (1.0 / seqs)
                 made = made.astype(BF16)
-                for k in range(step_pieces):
-                    for e in range(per):
-                        lane = (step * per + e) * LANES
-                        if not isinstance(lane, int):
-                            lane = pl.multiple_of(lane, LANES)
-                        lhs[
-                            base + (s + k) * count : base + (s + k + 1) * count, pl.ds(lane, LANES)
-                        ] = made[e * count : (e + 1) * count, k * LANES : (k + 1) * LANES]
+                for e in range(per):
+                    lane = (step * per + e) * LANES
+                    if not isinstance(lane, int):
+                        lane = pl.multiple_of(lane, LANES)
+                    for half in range(halves):
+                        row = base + (half * len(pieces) + s) * count
+                        lhs[row : row + count, pl.ds(lane, LANES)] = made[
+                            e * count : (e + 1) * count, half * LANES : (half + 1) * LANES
+                        ]
 
             for_chunks(rows // chunk, one)
             for _ in range(min(share, len(todo))):
                 fill(todo.pop())
 
-    share = -(-factor * 2 // (n_row + n_col))
-    direct = n_row * count_j
-    mirrored = n_col * count_i
+    share = -(-factor // (n_row + n_col))
+    direct = halves * n_row * count_j
+    mirrored = halves * n_col * count_i
     outer(a_c, count_j, row_refs, 0)
     outer(a_r, count_i, col_refs, direct)
-
     while todo:
         fill(todo.pop())
 
@@ -499,13 +489,19 @@
 
     lhs_out = grid[1]
     start = grid[0]
-    for_chunks(total // chunk, project)
+    if total == 2 * chunk:
+        project(0)
+        project(1)
+    else:
+        for_chunks(total // chunk, project)
     side_r = row_side.astype(F32)
     side_c = col_side.astype(F32)
     place = 0
     for slot in range(n_row):
         for r in range(n_res):
-            made = lhs_out[slot * count_j : (slot + 1) * count_j, r * LANES : (r + 1) * LANES]
+            row = (r // PAIR * n_row + slot) * count_j
+            lane = r % PAIR * LANES
+            made = lhs_out[row : row + count_j, lane : lane + LANES]
             left = side_r[slot * 16 + r : slot * 16 + r + 1, :]
             start[place : place + count_j, :] = (
                 (left + right_c) + rel_ref[place : place + count_j, :] + made
@@ -513,10 +509,9 @@
             place += count_j
     for slot in range(n_col):
         for r in range(n_res):
-            made = lhs_out[
-                direct + slot * count_i : direct + (slot + 1) * count_i,
-                r * LANES : (r + 1) * LANES,
-            ]
+            row = direct + (r // PAIR * n_col + slot) * count_i
+            lane = r % PAIR * LANES
+            made = lhs_out[row : row + count_i, lane : lane + LANES]
             left = side_c[slot * 16 + r : slot * 16 + r + 1, :]
             start[place : place + count_i, :] = (
                 (left + right_r) + rel_ref[place : place + count_i, :] + made
@@ -591,11 +586,11 @@
         leave.wait()
 
 
-def pair_grid(places, row_pieces, col_pieces, weights, large, n_res, seqs):
+def pair_grid(places, row_pieces, col_pieces, weights, n_res, seqs):
     n_row, n_col = len(row_pieces), len(col_pieces)
     count_i, count_j = n_row * n_res, n_col * n_res
     factor = LANES // n_res
-    total = n_row * count_j + n_col * count_i
+    total = (n_row * count_j + n_col * count_i) * n_res // PAIR
     cells = count_i * count_j
     n_bins = weights[2].shape[0]
     return local_call(
@@ -604,28 +599,26 @@
             jax.ShapeDtypeStruct((count_i, count_j, LANES), BF16),
             jax.ShapeDtypeStruct((count_i, count_j, n_bins), BF16),
         ),
-        in_specs=[VMEM] * (n_row + n_col + len(weights)) + [HBM] * len(large),
+        in_specs=[VMEM] * (n_row + n_col + len(weights)),
         out_specs=(HBM, HBM),
         scratch_shapes=[
-            pltpu.VMEM((factor * count_i, seqs), BF16),
-            pltpu.VMEM((factor * count_j, seqs), BF16),
-            pltpu.VMEM((total, factor * LANES), BF16),
+            pltpu.VMEM((factor // PAIR * count_i, PAIR * seqs), BF16),
+            pltpu.VMEM((factor // PAIR * count_j, PAIR * seqs), BF16),
+            pltpu.VMEM((total, factor // PAIR * LANES), BF16),
             (
                 pltpu.VMEM((2 * cells, LANES), F32),
-                pltpu.VMEM((total, n_res * LANES), F32),
+                pltpu.VMEM((total, PAIR * LANES), F32),
                 pltpu.VMEM((2 * cells, LANES), BF16),
                 pltpu.VMEM((2 * cells, n_bins), F32),
             ),
             pltpu.VMEM((cells, LANES), F32),
-            *[pltpu.VMEM(w.shape, BF16) for w in large],
-            pltpu.VMEM((factor * LANES, n_res * LANES), BF16),
+            pltpu.VMEM((factor // PAIR * LANES, PAIR * LANES), BF16),
             pltpu.VMEM((count_i, count_j, LANES), BF16),
             pltpu.VMEM((count_i, count_j, n_bins), BF16),
-            pltpu.SemaphoreType.DMA((len(large),)),
             pltpu.SemaphoreType.DMA((1 + n_row,)),
         ],
         name="pairs",
-    )(*[near(v) for v in (*row_pieces, *col_pieces, *weights)], *[far(w) for w in large])
+    )(*[near(v) for v in (*row_pieces, *col_pieces, *weights)])
 
 
 def plane_offsets(n_row, n_col):
@@ -705,8 +698,9 @@
             factors,
             row_amino_embedding,
             column_amino_embedding,
+            stack_transition_expand_matrix,
+            stack_transition_shrink_matrix,
         ),
-        (stack_transition_expand_matrix, stack_transition_shrink_matrix),
         (projection, relative),
         n_res,
     )
@@ -736,8 +730,10 @@
             relative,
             swap,
             distance_bins_matrix.T,
+            projection,
+            grid_transition_expand,
+            grid_transition_shrink,
         ),
-        (projection, grid_transition_expand, grid_transition_shrink),
         n_res,
         seqs,
     )

time: 44.3 us -> 42.7 us (0.964)
  Pallas kernels: 12.5 us -> 10.8 us
  waiting for transfers between devices: 9.66 us -> 10.3 us
  local copies, waits for them, and re-layouts: 3.32 us -> 2.75 us
    pallas_call x1, Pallas kernels: 5.27 us -> 3.8 us  [pair_grid(): local_call(functools.partial(pair_kernel, n_row, n_col, n_res, seqs, plac...]
    all_to_all x1, waiting for transfers between devices: 4.73 us -> 5.37 us  [shards(): moved = lax.all_to_all(sent, axes, split_axis=0, concat_axis=0, tiled=True)]
    unnamed x32 -> x42, local copies, waits for them, and re-layouts: 1.98 us -> 1.41 us
where the time goes in v1:
time: 42.7 us; the launch traced here: 42.3 us
  starting transfers between devices  17 us (40%)
  Pallas kernels  10.8 us (25%)
  waiting for transfers between devices  10.3 us (24%)
  local copies, waits for them, and re-layouts  2.75 us (6%)
  between operations  0.94 us (2%)
  other arithmetic  0.47 us (1%)
    all_to_all x1, starting transfers between devices, shards(): moved = lax.all_to_all(sent, axes, split_axis=0, concat_axis=0, tiled=True)  7.33 us
    all_to_all x1, waiting for transfers between devices, shards(): moved = lax.all_to_all(sent, axes, split_axis=0, concat_axis=0, tiled=True)  5.37 us
    ppermute x7, starting transfers between devices, along_col(): return lax.ppermute(value, 'col', [(c, c ^ m) for c in range(n_cols)])  5.28 us
    pallas_call x1, Pallas kernels, pair_grid(): local_call(functools.partial(pair_kernel, n_row, n_col, n_res, seqs, plac...  3.8 us
    ppermute x3, starting transfers between devices, along_row(): return lax.ppermute(value, 'row', [(r, r ^ m) for r in range(n_rows)])  3.48 us
    ppermute x1, waiting for transfers between devices, shards(): turned = lax.ppermute(piece, axes, turn)  3.27 us
    pallas_call x1, Pallas kernels, attention(): local_call(functools.partial(attention_kernel, n_res), out_shape=(pltpu.V...  3.14 us
    pallas_call x1, Pallas kernels, chunks(): local_call(functools.partial(chunk_kernel, n_res, parts), out_shape=pltpu...  1.65 us
  transfers between devices with their start and end apart: 12, of which 5 were waited for; matrix products, arithmetic and copies ran while one was open for 4% of the time, Pallas kernels for 5%

profile of v1, /device:TPU:0, one launch (start us, length us, event | category | flops | bytes accessed | tf_op | source)
XLA Modules:
  0.0 42.3 jit_solution(7977378944596425781)
XLA Ops:
  0.6 1.7 %chunks.1 = bf16[512,256]{1,0:T(8,128)(2,1)} custom-call(bf16[4,128,256]{2,1,0:T(8,128)(2,1)} %x_far.1), custom_call_target="tpu_custom_call" | custom-call | tf_op jit(solution)/shard_map/chunks/pallas_call | solution.py:108
  2.3 7.3 %all-to-all-start = ((bf16[32,16,256]{2,1,0:T(8,128)(2,1)}), bf16[32,16,256]{2,1,0:T(8,128)(2,1)S(1)}, u32[]{:S(2)}, u32[]{:S(2)}) async-start(bf16[32,16,256]{2,1,0:T(8,128)(2,1)} %bitcast.23), calls=%async_computation | async-start | bytes 524288 | tf_op jit(solution)/shard_map/all_to_all | solution.py:669
  9.7 0.2 broadcast_multiply_fusion
  9.9 0.2 copy.25
  10.1 0.5 %copy-done.17 = bf16[256,32]{0,1:T(8,128)(2,1)S(1)} copy-done((bf16[256,32]{0,1:T(8,128)(2,1)S(1)}, bf16[256,32]{0,1:T(8,128)(2,1)}, u32[]{:S(2)}) %copy-start.17) | copy-done | bytes 16408
  10.6 0.2 broadcast_multiply_fusion.1
  10.8 0.0 copy-start.5
  10.8 0.0 copy-start.15
  10.9 0.0 copy-start.14
  10.9 0.2 copy.24
  11.0 0.7 %copy-done.5 = bf16[1024,128]{1,0:T(8,128)(2,1)S(1)} copy-done((bf16[1024,128]{1,0:T(8,128)(2,1)S(1)}, bf16[1024,128]{1,0:T(8,128)(2,1)}, u32[]{:S(2)}) %copy-start.5) | copy-done | bytes 262168
  11.8 1.0 %turn.1._.refs_15_ = bf16[1024,128]{1,0:T(8,128)(2,1)} custom-call(bf16[1024,128]{1,0:T(8,128)(2,1)S(1)} %copy-done.5), custom_call_target="tpu_custom_call" | custom-call | tf_op jit(solution)/shard_map/turn/pallas_call | solution.py:133
  12.8 1.2 %relative.1 = (bf16[1024,128]{1,0:T(8,128)(2,1)}, bf16[512,512]{1,0:T(8,128)(2,1)}) custom-call(bf16[65,128]{1,0:T(8,128)(2,1)S(1)} %copy-done.15), custom_call_target="tpu_custom_call" | custom-call | tf_op jit(solution)/shard_map/relative/pallas_call | solution.py:348
  14.0 0.1 pad.4.clone
  14.1 0.1 pad_maximum_fusion.fg_ref
  14.2 0.1 maximum_maximum_fusion.amino_ref
  14.3 5.4 %all-to-all-done = bf16[32,16,256]{2,1,0:T(8,128)(2,1)S(1)} async-done(((bf16[32,16,256]{2,1,0:T(8,128)(2,1)}), bf16[32,16,256]{2,1,0:T(8,128)(2,1)S(1)}, u32[]{:S(2)}, u32[]{:S(2)}) %all-to-all-start) | async-done | bytes 262176 | tf_op jit(solution)/shard_map/all_to_all | solution.py:669
  19.7 0.0 copy-start.11
  19.7 0.0 copy-start.12
  19.8 3.1 %attention.1 = (bf16[512,256]{1,0:T(8,128)(2,1)S(1)}, bf16[272,128]{1,0:T(8,128)(2,1)S(1)}) custom-call(bf16[512,256]{1,0:T(8,128)(2,1)S(1)} %bitcast.20, bf16[16,256]{1,0:T(8,128)(2,1)S(1)} %maximum_maximum_fusion.amino_ref, bf16[256,256]{1,0:T(8,128)(2,1)S(1)} %copy-done.6, bf16[256,256]{1,0:T(8,128)(2,1)S(1)} %copy-done.7, ...), custom_call_target="tpu_custom_call" | custom-call | tf_op jit(solution)/shard_map/attention/pallas_call | solution.py:258
  22.9 0.9 %collective-permute-start.7 = (bf16[272,128]{1,0:T(8,128)(2,1)S(1)}, bf16[272,128]{1,0:T(8,128)(2,1)S(1)}, u32[]{:S(2)}, u32[]{:S(2)}) collective-permute-start(bf16[272,128]{1,0:T(8,128)(2,1)S(1)} %get-tuple-element.11.refs_0_), channel_id=1, source_target_pairs={{0,16},{1,24},{2,0},{3,8},{4,17},{5,25},{6,1},{7,9},{8,10},{9,2},{... | collective-permute-start | bytes 208904 | tf_op jit(solution)/shard_map/ppermute | solution.py:713
  23.8 0.4 collective-permute-start.3
  24.2 3.3 %collective-permute-start.2 = (bf16[272,128]{1,0:T(8,128)(2,1)S(1)}, bf16[272,128]{1,0:T(8,128)(2,1)S(1)}, u32[]{:S(2)}, u32[]{:S(2)}) collective-permute-start(bf16[272,128]{1,0:T(8,128)(2,1)S(1)} %get-tuple-element.11.refs_0_), channel_id=1, source_target_pairs={{0,6},{1,7},{2,4},{3,5},{4,2},{5,3},{6,0},{7,1},{8,14},{9,15},{10,... | collective-permute-start | bytes 208904 | tf_op jit(solution)/shard_map/ppermute | solution.py:716
  27.5 1.1 %collective-permute-start = (bf16[272,128]{1,0:T(8,128)(2,1)S(1)}, bf16[272,128]{1,0:T(8,128)(2,1)S(1)}, u32[]{:S(2)}, u32[]{:S(2)}) collective-permute-start(bf16[272,128]{1,0:T(8,128)(2,1)S(1)} %get-tuple-element.11.refs_0_), channel_id=1, source_target_pairs={{0,2},{1,3},{2,0},{3,1},{4,6},{5,7},{6,4},{7,5},{8,10},{9,11},{10,... | collective-permute-start | bytes 208904 | tf_op jit(solution)/shard_map/ppermute | solution.py:716
  28.6 3.3 %collective-permute-done.7.refs_8_ = bf16[272,128]{1,0:T(8,128)(2,1)S(1)} collective-permute-done((bf16[272,128]{1,0:T(8,128)(2,1)S(1)}, bf16[272,128]{1,0:T(8,128)(2,1)S(1)}, u32[]{:S(2)}, u32[]{:S(2)}) %collective-permute-start.7) | collective-permute-done | bytes 69664 | tf_op jit(solution)/shard_map/ppermute | solution.py:713
  31.9 3.5 %collective-permute-start.8 = (bf16[272,128]{1,0:T(8,128)(2,1)S(1)}, bf16[272,128]{1,0:T(8,128)(2,1)S(1)}, u32[]{:S(2)}, u32[]{:S(2)}) collective-permute-start(bf16[272,128]{1,0:T(8,128)(2,1)S(1)} %collective-permute-done.7.refs_8_), channel_id=1, source_target_pairs={{0,8},{8,0},{16,24},{24,16},{1,9},{9,1},{17,25},{25,17},{2,10},{10... | collective-permute-start | bytes 208904 | tf_op jit(solution)/shard_map/ppermute | solution.py:719
  35.4 1.0 %collective-permute-done.1.refs_2_ = bf16[272,128]{1,0:T(8,128)(2,1)S(1)} collective-permute-done((bf16[272,128]{1,0:T(8,128)(2,1)S(1)}, bf16[272,128]{1,0:T(8,128)(2,1)S(1)}, u32[]{:S(2)}, u32[]{:S(2)}) %collective-permute-start.1) | collective-permute-done | bytes 69664 | tf_op jit(solution)/shard_map/ppermute | solution.py:716
  36.4 0.5 %collective-permute-start.5 = (bf16[272,128]{1,0:T(8,128)(2,1)S(1)}, bf16[272,128]{1,0:T(8,128)(2,1)S(1)}, u32[]{:S(2)}, u32[]{:S(2)}) collective-permute-start(bf16[272,128]{1,0:T(8,128)(2,1)S(1)} %collective-permute-done.1.refs_2_), channel_id=1, source_target_pairs={{0,1},{1,0},{2,3},{3,2},{4,5},{5,4},{6,7},{7,6},{8,9},{9,8},{10,11... | collective-permute-start | bytes 208904 | tf_op jit(solution)/shard_map/ppermute | solution.py:716
  36.9 0.3 collective-permute-done.10.refs_11_
  37.2 0.9 %copy.30 = bf16[4,128,256]{2,0,1:T(4,128)(2,1)} copy(bf16[4,128,256]{2,1,0:T(8,128)(2,1)S(1)} %bitcast.21) | data formatting | bytes 524288 | tf_op jit(solution)/shard_map/reshape | solution.py:707
  38.1 0.3 collective-permute-done.4.refs_5_
  38.5 3.8 %pairs.1 = (bf16[32,16,128]{2,1,0:T(8,128)(2,1)}, bf16[32,16,64]{2,1,0:T(8,128)(2,1)}) custom-call(bf16[272,128]{1,0:T(8,128)(2,1)S(1)} %get-tuple-element.11.refs_0_, bf16[272,128]{1,0:T(8,128)(2,1)S(1)} %collective-permute-done.refs_1_, bf16[272,128]{1,0:T(8,128)(2,1)S(1)} %collective-permute-done.1.refs_2_, ...), custom_call_target="tpu_custom_call" | custom-call | tf_op jit(solution)/shard_map/pairs/pallas_call | solution.py:596
  (50 shorter events, 0.2 us)
Async XLA Ops:
  2.3 7.4 %copy-start.18 = (bf16[256,32]{0,1:T(8,128)(2,1)S(1)}, bf16[256,32]{0,1:T(8,128)(2,1)}, u32[]{:S(2)}) copy-start(bf16[256,32]{0,1:T(8,128)(2,1)} %param.28) | copy-start | bytes 49156
  2.3 17.3 %all-to-all-start = ((bf16[32,16,256]{2,1,0:T(8,128)(2,1)}), bf16[32,16,256]{2,1,0:T(8,128)(2,1)S(1)}, u32[]{:S(2)}, u32[]{:S(2)}) async-start(bf16[32,16,256]{2,1,0:T(8,128)(2,1)} %bitcast.23), calls=%async_computation | async-start | bytes 524288 | tf_op jit(solution)/shard_map/all_to_all | solution.py:669
  9.9 0.7 %copy-start.17 = (bf16[256,32]{0,1:T(8,128)(2,1)S(1)}, bf16[256,32]{0,1:T(8,128)(2,1)}, u32[]{:S(2)}) copy-start(bf16[256,32]{0,1:T(8,128)(2,1)} %param.27) | copy-start | bytes 49156
  10.8 1.0 %copy-start.5 = (bf16[1024,128]{1,0:T(8,128)(2,1)S(1)}, bf16[1024,128]{1,0:T(8,128)(2,1)}, u32[]{:S(2)}) copy-start(bf16[1024,128]{1,0:T(8,128)(2,1)} %w_ref.1) | copy-start | bytes 786436
  10.8 2.0 %copy-start.15 = (bf16[65,128]{1,0:T(8,128)(2,1)S(1)}, bf16[65,128]{1,0:T(8,128)(2,1)}, u32[]{:S(2)}) copy-start(bf16[65,128]{1,0:T(8,128)(2,1)} %off_ref.1) | copy-start | bytes 49924
  10.8 8.8 %copy-start.10 = (bf16[256,256]{1,0:T(8,128)(2,1)S(1)}, bf16[256,256]{1,0:T(8,128)(2,1)}, u32[]{:S(2)}) copy-start(bf16[256,256]{1,0:T(8,128)(2,1)} %wo_ref.1) | copy-start | bytes 393220
  10.8 8.8 %copy-start.13 = (bf16[256,128]{1,0:T(8,128)(2,1)S(1)}, bf16[256,128]{1,0:T(8,128)(2,1)}, u32[]{:S(2)}) copy-start(bf16[256,128]{1,0:T(8,128)(2,1)} %re_ref.1) | copy-start | bytes 196612
  10.9 8.8 %copy-start.14 = (bf16[256,128]{1,0:T(8,128)(2,1)S(1)}, bf16[256,128]{1,0:T(8,128)(2,1)}, u32[]{:S(2)}) copy-start(bf16[256,128]{1,0:T(8,128)(2,1)} %ce_ref.1) | copy-start | bytes 196612
  11.8 2.4 %copy-start.19 = (bf16[4,256]{1,0:T(4,128)(2,1)S(1)}, bf16[4,256]{1,0:T(4,128)(2,1)}, u32[]{:S(2)}) copy-start(bf16[4,256]{1,0:T(4,128)(2,1)} %param.19) | copy-start | bytes 6148
  11.8 7.9 %copy-start.6 = (bf16[256,256]{1,0:T(8,128)(2,1)S(1)}, bf16[256,256]{1,0:T(8,128)(2,1)}, u32[]{:S(2)}) copy-start(bf16[256,256]{1,0:T(8,128)(2,1)} %wq_ref.1) | copy-start | bytes 393220
  11.8 7.9 %copy-start.7 = (bf16[256,256]{1,0:T(8,128)(2,1)S(1)}, bf16[256,256]{1,0:T(8,128)(2,1)}, u32[]{:S(2)}) copy-start(bf16[256,256]{1,0:T(8,128)(2,1)} %wk_ref.1) | copy-start | bytes 393220
  11.8 7.9 %copy-start.8 = (bf16[256,256]{1,0:T(8,128)(2,1)S(1)}, bf16[256,256]{1,0:T(8,128)(2,1)}, u32[]{:S(2)}) copy-start(bf16[256,256]{1,0:T(8,128)(2,1)} %wv_ref.1) | copy-start | bytes 393220
  11.8 7.9 %copy-start.9 = (bf16[256,256]{1,0:T(8,128)(2,1)S(1)}, bf16[256,256]{1,0:T(8,128)(2,1)}, u32[]{:S(2)}) copy-start(bf16[256,256]{1,0:T(8,128)(2,1)} %wg_ref.1) | copy-start | bytes 393220
  14.1 5.6 %copy-start.2 = (bf16[256,1024]{1,0:T(8,128)(2,1)S(1)}, bf16[256,1024]{1,0:T(8,128)(2,1)}, u32[]{:S(2)}) copy-start(bf16[256,1024]{1,0:T(8,128)(2,1)} %w1_ref.1) | copy-start | bytes 1572868
  14.1 5.6 %copy-start.3 = (bf16[1024,256]{1,0:T(8,128)(2,1)S(1)}, bf16[1024,256]{1,0:T(8,128)(2,1)}, u32[]{:S(2)}) copy-start(bf16[1024,256]{1,0:T(8,128)(2,1)} %w2_ref.1) | copy-start | bytes 1572868
  19.7 18.7 %copy-start.4 = (bf16[512,512]{1,0:T(8,128)(2,1)S(1)}, bf16[512,512]{1,0:T(8,128)(2,1)}, u32[]{:S(2)}) copy-start(bf16[512,512]{1,0:T(8,128)(2,1)} %get-tuple-element.12.refs_13_) | copy-start | bytes 1572868
  19.7 18.7 %copy-start.11 = (bf16[128,512]{1,0:T(8,128)(2,1)S(1)}, bf16[128,512]{1,0:T(8,128)(2,1)}, u32[]{:S(2)}) copy-start(bf16[128,512]{1,0:T(8,128)(2,1)} %refs_16_.1) | copy-start | bytes 393220
  19.7 18.7 %copy-start.12 = (bf16[512,128]{1,0:T(8,128)(2,1)S(1)}, bf16[512,128]{1,0:T(8,128)(2,1)}, u32[]{:S(2)}) copy-start(bf16[512,128]{1,0:T(8,128)(2,1)} %refs_17_.1) | copy-start | bytes 393220
  19.7 18.7 %copy-start.16 = (bf16[128,64]{0,1:T(8,128)(2,1)S(1)}, bf16[128,64]{0,1:T(8,128)(2,1)}, u32[]{:S(2)}) copy-start(bf16[128,64]{0,1:T(8,128)(2,1)} %param.35) | copy-start | bytes 49156
  22.9 9.0 %collective-permute-start.7 = (bf16[272,128]{1,0:T(8,128)(2,1)S(1)}, bf16[272,128]{1,0:T(8,128)(2,1)S(1)}, u32[]{:S(2)}, u32[]{:S(2)}) collective-permute-start(bf16[272,128]{1,0:T(8,128)(2,1)S(1)} %get-tuple-element.11.refs_0_), channel_id=1, source_target_pairs={{0,16},{1,24},{2,0},{3,8},{4,17},{5,25},{6,1},{7,9},{8,10},{9,2},{... | collective-permute-start | bytes 208904 | tf_op jit(solution)/shard_map/ppermute | solution.py:713
  23.8 8.0 %collective-permute-start.3 = (bf16[272,128]{1,0:T(8,128)(2,1)S(1)}, bf16[272,128]{1,0:T(8,128)(2,1)S(1)}, u32[]{:S(2)}, u32[]{:S(2)}) collective-permute-start(bf16[272,128]{1,0:T(8,128)(2,1)S(1)} %get-tuple-element.11.refs_0_), channel_id=1, source_target_pairs={{0,1},{1,0},{2,3},{3,2},{4,5},{5,4},{6,7},{7,6},{8,9},{9,8},{10,11... | collective-permute-start | bytes 208904 | tf_op jit(solution)/shard_map/ppermute | solution.py:716
  24.2 7.7 %collective-permute-start.2 = (bf16[272,128]{1,0:T(8,128)(2,1)S(1)}, bf16[272,128]{1,0:T(8,128)(2,1)S(1)}, u32[]{:S(2)}, u32[]{:S(2)}) collective-permute-start(bf16[272,128]{1,0:T(8,128)(2,1)S(1)} %get-tuple-element.11.refs_0_), channel_id=1, source_target_pairs={{0,6},{1,7},{2,4},{3,5},{4,2},{5,3},{6,0},{7,1},{8,14},{9,15},{10,... | collective-permute-start | bytes 208904 | tf_op jit(solution)/shard_map/ppermute | solution.py:716
  27.5 8.9 %collective-permute-start.1 = (bf16[272,128]{1,0:T(8,128)(2,1)S(1)}, bf16[272,128]{1,0:T(8,128)(2,1)S(1)}, u32[]{:S(2)}, u32[]{:S(2)}) collective-permute-start(bf16[272,128]{1,0:T(8,128)(2,1)S(1)} %get-tuple-element.11.refs_0_), channel_id=1, source_target_pairs={{0,4},{1,5},{2,6},{3,7},{4,0},{5,1},{6,2},{7,3},{8,12},{9,13},{10,... | collective-permute-start | bytes 208904 | tf_op jit(solution)/shard_map/ppermute | solution.py:716
  27.5 8.9 %collective-permute-start = (bf16[272,128]{1,0:T(8,128)(2,1)S(1)}, bf16[272,128]{1,0:T(8,128)(2,1)S(1)}, u32[]{:S(2)}, u32[]{:S(2)}) collective-permute-start(bf16[272,128]{1,0:T(8,128)(2,1)S(1)} %get-tuple-element.11.refs_0_), channel_id=1, source_target_pairs={{0,2},{1,3},{2,0},{3,1},{4,6},{5,7},{6,4},{7,5},{8,10},{9,11},{10,... | collective-permute-start | bytes 208904 | tf_op jit(solution)/shard_map/ppermute | solution.py:716
  31.9 5.3 %collective-permute-start.10 = (bf16[272,128]{1,0:T(8,128)(2,1)S(1)}, bf16[272,128]{1,0:T(8,128)(2,1)S(1)}, u32[]{:S(2)}, u32[]{:S(2)}) collective-permute-start(bf16[272,128]{1,0:T(8,128)(2,1)S(1)} %collective-permute-done.7.refs_8_), channel_id=1, source_target_pairs={{0,24},{8,16},{16,8},{24,0},{1,25},{9,17},{17,9},{25,1},{2,26},{10... | collective-permute-start | bytes 208904 | tf_op jit(solution)/shard_map/ppermute | solution.py:719
  31.9 6.2 %collective-permute-start.9 = (bf16[272,128]{1,0:T(8,128)(2,1)S(1)}, bf16[272,128]{1,0:T(8,128)(2,1)S(1)}, u32[]{:S(2)}, u32[]{:S(2)}) collective-permute-start(bf16[272,128]{1,0:T(8,128)(2,1)S(1)} %collective-permute-done.7.refs_8_), channel_id=1, source_target_pairs={{0,16},{8,24},{16,0},{24,8},{1,17},{9,25},{17,1},{25,9},{2,18},{10... | collective-permute-start | bytes 208904 | tf_op jit(solution)/shard_map/ppermute | solution.py:719
  31.9 6.2 %collective-permute-start.8 = (bf16[272,128]{1,0:T(8,128)(2,1)S(1)}, bf16[272,128]{1,0:T(8,128)(2,1)S(1)}, u32[]{:S(2)}, u32[]{:S(2)}) collective-permute-start(bf16[272,128]{1,0:T(8,128)(2,1)S(1)} %collective-permute-done.7.refs_8_), channel_id=1, source_target_pairs={{0,8},{8,0},{16,24},{24,16},{1,9},{9,1},{17,25},{25,17},{2,10},{10... | collective-permute-start | bytes 208904 | tf_op jit(solution)/shard_map/ppermute | solution.py:719
  36.4 1.7 %collective-permute-start.6 = (bf16[272,128]{1,0:T(8,128)(2,1)S(1)}, bf16[272,128]{1,0:T(8,128)(2,1)S(1)}, u32[]{:S(2)}, u32[]{:S(2)}) collective-permute-start(bf16[272,128]{1,0:T(8,128)(2,1)S(1)} %collective-permute-done.2.refs_3_), channel_id=1, source_target_pairs={{0,1},{1,0},{2,3},{3,2},{4,5},{5,4},{6,7},{7,6},{8,9},{9,8},{10,11... | collective-permute-start | bytes 208904 | tf_op jit(solution)/shard_map/ppermute | solution.py:716
  36.4 1.7 %collective-permute-start.5 = (bf16[272,128]{1,0:T(8,128)(2,1)S(1)}, bf16[272,128]{1,0:T(8,128)(2,1)S(1)}, u32[]{:S(2)}, u32[]{:S(2)}) collective-permute-start(bf16[272,128]{1,0:T(8,128)(2,1)S(1)} %collective-permute-done.1.refs_2_), channel_id=1, source_target_pairs={{0,1},{1,0},{2,3},{3,2},{4,5},{5,4},{6,7},{7,6},{8,9},{9,8},{10,11... | collective-permute-start | bytes 208904 | tf_op jit(solution)/shard_map/ppermute | solution.py:716
  37.2 1.3 %collective-permute-start.4 = (bf16[272,128]{1,0:T(8,128)(2,1)S(1)}, bf16[272,128]{1,0:T(8,128)(2,1)S(1)}, u32[]{:S(2)}, u32[]{:S(2)}) collective-permute-start(bf16[272,128]{1,0:T(8,128)(2,1)S(1)} %collective-permute-done.refs_1_), channel_id=1, source_target_pairs={{0,1},{1,0},{2,3},{3,2},{4,5},{5,4},{6,7},{7,6},{8,9},{9,8},{10,11... | collective-permute-start | bytes 208904 | tf_op jit(solution)/shard_map/ppermute | solution.py:716
  37.2 1.3 %copy-start = (bf16[1024,128]{1,0:T(8,128)(2,1)S(1)}, bf16[1024,128]{1,0:T(8,128)(2,1)}, u32[]{:S(2)}) copy-start(bf16[1024,128]{1,0:T(8,128)(2,1)} %turn.1._.refs_15_) | copy-start | bytes 786436
  37.2 1.3 %copy-start.1 = (bf16[1024,128]{1,0:T(8,128)(2,1)S(1)}, bf16[1024,128]{1,0:T(8,128)(2,1)}, u32[]{:S(2)}) copy-start(bf16[1024,128]{1,0:T(8,128)(2,1)} %get-tuple-element.9._2.refs_12_) | copy-start | bytes 786436

commit v2 on v1

--- a/solution.py
+++ b/solution.py
@@ -215,27 +215,29 @@
         summed = dot(values, jnp.concatenate(powers, axis=0)) * jnp.concatenate(inverse, axis=0)
         mix_scr[at, lanes] = (summed.T * g_scr[at, lanes]).astype(BF16)
 
-    if seqs <= LANES:
-        for i in range(n_res):
-            for tile in range(tiles):
-                attend(i, tile)
-    else:
-
-        def attend_all(i):
-            for tile in range(tiles):
-                attend(i, tile)
-
-        for_chunks(n_res, attend_all)
+    block = 2 * seqs if seqs <= LANES else chunk
 
     def transition(step):
-        at = rows_at(step * chunk, chunk)
+        at = rows_at(step * block, block)
         first = res_scr[at, :] + dot(mix_scr[at, :], wo_ref[...])
         hidden = jnp.maximum(dot(standardize(first).astype(BF16), w1_ref[...]), 0.0).astype(BF16)
         second = first + dot(hidden, w2_ref[...])
         align_ref[at, :] = second.astype(BF16)
         ln_scr[at, :] = standardize(second).astype(BF16)
 
-    for_chunks(rows // chunk, transition)
+    if seqs <= LANES:
+        for i in range(n_res):
+            for tile in range(tiles):
+                attend(i, tile)
+        for step in range(n_res // 2):
+            transition(step)
+    else:
+        def attend_all(i):
+            for tile in range(tiles):
+                attend(i, tile)
+
+        for_chunks(n_res, attend_all)
+        for_chunks(rows // block, transition)
 
     side = jnp.concatenate([ln_scr[i * seqs : (i + 1) * seqs, :] for i in range(n_res)], axis=1)
     factors = dot(side, fg_ref[...])
@@ -718,8 +720,10 @@
     def along_row(value, m):
         return lax.ppermute(value, "row", [(r, r ^ m) for r in range(n_rows)])
 
+
     own = [piece] + [along_col(piece, 2 * m) for m in range(1, n_cols // 2)]
-    other = [along_col(value, 1) for value in own]
+    other = [along_col(value, 1) for value in own[1:]]
+    other = [along_col(piece, 1)] + other
     col_pieces = [turned] + [along_row(turned, m) for m in range(1, n_rows)]
 
     pair_output, distogram = pair_grid(

time: 42.7 us -> 42.5 us (level)
  no operation moved by 1% of the time
where the time goes in v2:
time: 42.5 us; the launch traced here: 42.1 us
  starting transfers between devices  17 us (40%)
  Pallas kernels  10.6 us (25%)
  waiting for transfers between devices  10.3 us (24%)
  local copies, waits for them, and re-layouts  2.75 us (6%)
  between operations  0.94 us (2%)
  other arithmetic  0.47 us (1%)
    all_to_all x1, starting transfers between devices, shards(): moved = lax.all_to_all(sent, axes, split_axis=0, concat_axis=0, tiled=True)  7.33 us
    all_to_all x1, waiting for transfers between devices, shards(): moved = lax.all_to_all(sent, axes, split_axis=0, concat_axis=0, tiled=True)  5.37 us
    ppermute x7, starting transfers between devices, along_col(): return lax.ppermute(value, 'col', [(c, c ^ m) for c in range(n_cols)])  5.27 us
    pallas_call x1, Pallas kernels, pair_grid(): local_call(functools.partial(pair_kernel, n_row, n_col, n_res, seqs, plac...  3.8 us
    ppermute x3, starting transfers between devices, along_row(): return lax.ppermute(value, 'row', [(r, r ^ m) for r in range(n_rows)])  3.48 us
    ppermute x1, waiting for transfers between devices, shards(): turned = lax.ppermute(piece, axes, turn)  3.28 us
    pallas_call x1, Pallas kernels, attention(): local_call(functools.partial(attention_kernel, n_res), out_shape=(pltpu.V...  2.94 us
    pallas_call x1, Pallas kernels, chunks(): local_call(functools.partial(chunk_kernel, n_res, parts), out_shape=pltpu...  1.65 us
  transfers between devices with their start and end apart: 12, of which 5 were waited for; matrix products, arithmetic and copies ran while one was open for 4% of the time, Pallas kernels for 5%

profile of v2, /device:TPU:0, one launch (start us, length us, event | category | flops | bytes accessed | tf_op | source)
XLA Modules:
  0.0 42.1 jit_solution(2309857318295310338)
XLA Ops:
  0.6 1.7 %chunks.1 = bf16[512,256]{1,0:T(8,128)(2,1)} custom-call(bf16[4,128,256]{2,1,0:T(8,128)(2,1)} %x_far.1), custom_call_target="tpu_custom_call" | custom-call | tf_op jit(solution)/shard_map/chunks/pallas_call | solution.py:108
  2.3 7.3 %all-to-all-start = ((bf16[32,16,256]{2,1,0:T(8,128)(2,1)}), bf16[32,16,256]{2,1,0:T(8,128)(2,1)S(1)}, u32[]{:S(2)}, u32[]{:S(2)}) async-start(bf16[32,16,256]{2,1,0:T(8,128)(2,1)} %bitcast.23), calls=%async_computation | async-start | bytes 524288 | tf_op jit(solution)/shard_map/all_to_all | solution.py:671
  9.7 0.2 broadcast_multiply_fusion
  9.9 0.2 copy.25
  10.1 0.5 %copy-done.17 = bf16[256,32]{0,1:T(8,128)(2,1)S(1)} copy-done((bf16[256,32]{0,1:T(8,128)(2,1)S(1)}, bf16[256,32]{0,1:T(8,128)(2,1)}, u32[]{:S(2)}) %copy-start.17) | copy-done | bytes 16408
  10.6 0.2 broadcast_multiply_fusion.1
  10.8 0.0 copy-start.5
  10.8 0.0 copy-start.15
  10.9 0.0 copy-start.14
  10.9 0.2 copy.24
  11.0 0.7 %copy-done.5 = bf16[1024,128]{1,0:T(8,128)(2,1)S(1)} copy-done((bf16[1024,128]{1,0:T(8,128)(2,1)S(1)}, bf16[1024,128]{1,0:T(8,128)(2,1)}, u32[]{:S(2)}) %copy-start.5) | copy-done | bytes 262168
  11.8 1.0 %turn.1._.refs_15_ = bf16[1024,128]{1,0:T(8,128)(2,1)} custom-call(bf16[1024,128]{1,0:T(8,128)(2,1)S(1)} %copy-done.5), custom_call_target="tpu_custom_call" | custom-call | tf_op jit(solution)/shard_map/turn/pallas_call | solution.py:133
  12.8 1.2 %relative.1 = (bf16[1024,128]{1,0:T(8,128)(2,1)}, bf16[512,512]{1,0:T(8,128)(2,1)}) custom-call(bf16[65,128]{1,0:T(8,128)(2,1)S(1)} %copy-done.15), custom_call_target="tpu_custom_call" | custom-call | tf_op jit(solution)/shard_map/relative/pallas_call | solution.py:350
  14.0 0.1 pad.4.clone
  14.1 0.1 pad_maximum_fusion.fg_ref
  14.2 0.1 maximum_maximum_fusion.amino_ref
  14.3 5.4 %all-to-all-done = bf16[32,16,256]{2,1,0:T(8,128)(2,1)S(1)} async-done(((bf16[32,16,256]{2,1,0:T(8,128)(2,1)}), bf16[32,16,256]{2,1,0:T(8,128)(2,1)S(1)}, u32[]{:S(2)}, u32[]{:S(2)}) %all-to-all-start) | async-done | bytes 262176 | tf_op jit(solution)/shard_map/all_to_all | solution.py:671
  19.7 0.0 copy-start.11
  19.7 0.0 copy-start.12
  19.8 2.9 %attention.1 = (bf16[512,256]{1,0:T(8,128)(2,1)S(1)}, bf16[272,128]{1,0:T(8,128)(2,1)S(1)}) custom-call(bf16[512,256]{1,0:T(8,128)(2,1)S(1)} %bitcast.20, bf16[16,256]{1,0:T(8,128)(2,1)S(1)} %maximum_maximum_fusion.amino_ref, bf16[256,256]{1,0:T(8,128)(2,1)S(1)} %copy-done.6, bf16[256,256]{1,0:T(8,128)(2,1)S(1)} %copy-done.7, ...), custom_call_target="tpu_custom_call" | custom-call | tf_op jit(solution)/shard_map/attention/pallas_call | solution.py:260
  22.7 0.9 %collective-permute-start.7 = (bf16[272,128]{1,0:T(8,128)(2,1)S(1)}, bf16[272,128]{1,0:T(8,128)(2,1)S(1)}, u32[]{:S(2)}, u32[]{:S(2)}) collective-permute-start(bf16[272,128]{1,0:T(8,128)(2,1)S(1)} %get-tuple-element.11.refs_0_), channel_id=1, source_target_pairs={{0,16},{1,24},{2,0},{3,8},{4,17},{5,25},{6,1},{7,9},{8,10},{9,2},{... | collective-permute-start | bytes 208904 | tf_op jit(solution)/shard_map/ppermute | solution.py:715
  23.6 0.4 collective-permute-start.3
  24.0 3.3 %collective-permute-start.2 = (bf16[272,128]{1,0:T(8,128)(2,1)S(1)}, bf16[272,128]{1,0:T(8,128)(2,1)S(1)}, u32[]{:S(2)}, u32[]{:S(2)}) collective-permute-start(bf16[272,128]{1,0:T(8,128)(2,1)S(1)} %get-tuple-element.11.refs_0_), channel_id=1, source_target_pairs={{0,6},{1,7},{2,4},{3,5},{4,2},{5,3},{6,0},{7,1},{8,14},{9,15},{10,... | collective-permute-start | bytes 208904 | tf_op jit(solution)/shard_map/ppermute | solution.py:718
  27.3 1.1 %collective-permute-start = (bf16[272,128]{1,0:T(8,128)(2,1)S(1)}, bf16[272,128]{1,0:T(8,128)(2,1)S(1)}, u32[]{:S(2)}, u32[]{:S(2)}) collective-permute-start(bf16[272,128]{1,0:T(8,128)(2,1)S(1)} %get-tuple-element.11.refs_0_), channel_id=1, source_target_pairs={{0,2},{1,3},{2,0},{3,1},{4,6},{5,7},{6,4},{7,5},{8,10},{9,11},{10,... | collective-permute-start | bytes 208904 | tf_op jit(solution)/shard_map/ppermute | solution.py:718
  28.4 3.3 %collective-permute-done.7.refs_8_ = bf16[272,128]{1,0:T(8,128)(2,1)S(1)} collective-permute-done((bf16[272,128]{1,0:T(8,128)(2,1)S(1)}, bf16[272,128]{1,0:T(8,128)(2,1)S(1)}, u32[]{:S(2)}, u32[]{:S(2)}) %collective-permute-start.7) | collective-permute-done | bytes 69664 | tf_op jit(solution)/shard_map/ppermute | solution.py:715
  31.7 3.5 %collective-permute-start.8 = (bf16[272,128]{1,0:T(8,128)(2,1)S(1)}, bf16[272,128]{1,0:T(8,128)(2,1)S(1)}, u32[]{:S(2)}, u32[]{:S(2)}) collective-permute-start(bf16[272,128]{1,0:T(8,128)(2,1)S(1)} %collective-permute-done.7.refs_8_), channel_id=1, source_target_pairs={{0,8},{8,0},{16,24},{24,16},{1,9},{9,1},{17,25},{25,17},{2,10},{10... | collective-permute-start | bytes 208904 | tf_op jit(solution)/shard_map/ppermute | solution.py:721
  35.2 1.0 %collective-permute-done.1.refs_2_ = bf16[272,128]{1,0:T(8,128)(2,1)S(1)} collective-permute-done((bf16[272,128]{1,0:T(8,128)(2,1)S(1)}, bf16[272,128]{1,0:T(8,128)(2,1)S(1)}, u32[]{:S(2)}, u32[]{:S(2)}) %collective-permute-start.1) | collective-permute-done | bytes 69664 | tf_op jit(solution)/shard_map/ppermute | solution.py:718
  36.2 0.5 %collective-permute-start.5 = (bf16[272,128]{1,0:T(8,128)(2,1)S(1)}, bf16[272,128]{1,0:T(8,128)(2,1)S(1)}, u32[]{:S(2)}, u32[]{:S(2)}) collective-permute-start(bf16[272,128]{1,0:T(8,128)(2,1)S(1)} %collective-permute-done.1.refs_2_), channel_id=1, source_target_pairs={{0,1},{1,0},{2,3},{3,2},{4,5},{5,4},{6,7},{7,6},{8,9},{9,8},{10,11... | collective-permute-start | bytes 208904 | tf_op jit(solution)/shard_map/ppermute | solution.py:718
  36.7 0.3 collective-permute-done.10.refs_11_
  37.0 0.9 %copy.30 = bf16[4,128,256]{2,0,1:T(4,128)(2,1)} copy(bf16[4,128,256]{2,1,0:T(8,128)(2,1)S(1)} %bitcast.21) | data formatting | bytes 524288 | tf_op jit(solution)/shard_map/reshape | solution.py:709
  37.9 0.3 collective-permute-done.4.refs_5_
  38.3 3.8 %pairs.1 = (bf16[32,16,128]{2,1,0:T(8,128)(2,1)}, bf16[32,16,64]{2,1,0:T(8,128)(2,1)}) custom-call(bf16[272,128]{1,0:T(8,128)(2,1)S(1)} %get-tuple-element.11.refs_0_, bf16[272,128]{1,0:T(8,128)(2,1)S(1)} %collective-permute-done.refs_1_, bf16[272,128]{1,0:T(8,128)(2,1)S(1)} %collective-permute-done.1.refs_2_, ...), custom_call_target="tpu_custom_call" | custom-call | tf_op jit(solution)/shard_map/pairs/pallas_call | solution.py:598
  (50 shorter events, 0.2 us)
Async XLA Ops:
  2.3 7.4 %copy-start.18 = (bf16[256,32]{0,1:T(8,128)(2,1)S(1)}, bf16[256,32]{0,1:T(8,128)(2,1)}, u32[]{:S(2)}) copy-start(bf16[256,32]{0,1:T(8,128)(2,1)} %param.28) | copy-start | bytes 49156
  2.3 17.3 %all-to-all-start = ((bf16[32,16,256]{2,1,0:T(8,128)(2,1)}), bf16[32,16,256]{2,1,0:T(8,128)(2,1)S(1)}, u32[]{:S(2)}, u32[]{:S(2)}) async-start(bf16[32,16,256]{2,1,0:T(8,128)(2,1)} %bitcast.23), calls=%async_computation | async-start | bytes 524288 | tf_op jit(solution)/shard_map/all_to_all | solution.py:671
  9.9 0.7 %copy-start.17 = (bf16[256,32]{0,1:T(8,128)(2,1)S(1)}, bf16[256,32]{0,1:T(8,128)(2,1)}, u32[]{:S(2)}) copy-start(bf16[256,32]{0,1:T(8,128)(2,1)} %param.27) | copy-start | bytes 49156
  10.8 1.0 %copy-start.5 = (bf16[1024,128]{1,0:T(8,128)(2,1)S(1)}, bf16[1024,128]{1,0:T(8,128)(2,1)}, u32[]{:S(2)}) copy-start(bf16[1024,128]{1,0:T(8,128)(2,1)} %w_ref.1) | copy-start | bytes 786436
  10.8 2.0 %copy-start.15 = (bf16[65,128]{1,0:T(8,128)(2,1)S(1)}, bf16[65,128]{1,0:T(8,128)(2,1)}, u32[]{:S(2)}) copy-start(bf16[65,128]{1,0:T(8,128)(2,1)} %off_ref.1) | copy-start | bytes 49924
  10.8 8.8 %copy-start.10 = (bf16[256,256]{1,0:T(8,128)(2,1)S(1)}, bf16[256,256]{1,0:T(8,128)(2,1)}, u32[]{:S(2)}) copy-start(bf16[256,256]{1,0:T(8,128)(2,1)} %wo_ref.1) | copy-start | bytes 393220
  10.8 8.8 %copy-start.13 = (bf16[256,128]{1,0:T(8,128)(2,1)S(1)}, bf16[256,128]{1,0:T(8,128)(2,1)}, u32[]{:S(2)}) copy-start(bf16[256,128]{1,0:T(8,128)(2,1)} %re_ref.1) | copy-start | bytes 196612
  10.9 8.8 %copy-start.14 = (bf16[256,128]{1,0:T(8,128)(2,1)S(1)}, bf16[256,128]{1,0:T(8,128)(2,1)}, u32[]{:S(2)}) copy-start(bf16[256,128]{1,0:T(8,128)(2,1)} %ce_ref.1) | copy-start | bytes 196612
  11.8 2.4 %copy-start.19 = (bf16[4,256]{1,0:T(4,128)(2,1)S(1)}, bf16[4,256]{1,0:T(4,128)(2,1)}, u32[]{:S(2)}) copy-start(bf16[4,256]{1,0:T(4,128)(2,1)} %param.19) | copy-start | bytes 6148
  11.8 7.9 %copy-start.6 = (bf16[256,256]{1,0:T(8,128)(2,1)S(1)}, bf16[256,256]{1,0:T(8,128)(2,1)}, u32[]{:S(2)}) copy-start(bf16[256,256]{1,0:T(8,128)(2,1)} %wq_ref.1) | copy-start | bytes 393220
  11.8 7.9 %copy-start.7 = (bf16[256,256]{1,0:T(8,128)(2,1)S(1)}, bf16[256,256]{1,0:T(8,128)(2,1)}, u32[]{:S(2)}) copy-start(bf16[256,256]{1,0:T(8,128)(2,1)} %wk_ref.1) | copy-start | bytes 393220
  11.8 7.9 %copy-start.8 = (bf16[256,256]{1,0:T(8,128)(2,1)S(1)}, bf16[256,256]{1,0:T(8,128)(2,1)}, u32[]{:S(2)}) copy-start(bf16[256,256]{1,0:T(8,128)(2,1)} %wv_ref.1) | copy-start | bytes 393220
  11.8 7.9 %copy-start.9 = (bf16[256,256]{1,0:T(8,128)(2,1)S(1)}, bf16[256,256]{1,0:T(8,128)(2,1)}, u32[]{:S(2)}) copy-start(bf16[256,256]{1,0:T(8,128)(2,1)} %wg_ref.1) | copy-start | bytes 393220
  14.1 5.6 %copy-start.2 = (bf16[256,1024]{1,0:T(8,128)(2,1)S(1)}, bf16[256,1024]{1,0:T(8,128)(2,1)}, u32[]{:S(2)}) copy-start(bf16[256,1024]{1,0:T(8,128)(2,1)} %w1_ref.1) | copy-start | bytes 1572868
  14.1 5.6 %copy-start.3 = (bf16[1024,256]{1,0:T(8,128)(2,1)S(1)}, bf16[1024,256]{1,0:T(8,128)(2,1)}, u32[]{:S(2)}) copy-start(bf16[1024,256]{1,0:T(8,128)(2,1)} %w2_ref.1) | copy-start | bytes 1572868
  19.7 18.6 %copy-start.4 = (bf16[512,512]{1,0:T(8,128)(2,1)S(1)}, bf16[512,512]{1,0:T(8,128)(2,1)}, u32[]{:S(2)}) copy-start(bf16[512,512]{1,0:T(8,128)(2,1)} %get-tuple-element.12.refs_13_) | copy-start | bytes 1572868
  19.7 18.5 %copy-start.11 = (bf16[128,512]{1,0:T(8,128)(2,1)S(1)}, bf16[128,512]{1,0:T(8,128)(2,1)}, u32[]{:S(2)}) copy-start(bf16[128,512]{1,0:T(8,128)(2,1)} %refs_16_.1) | copy-start | bytes 393220
  19.7 18.5 %copy-start.12 = (bf16[512,128]{1,0:T(8,128)(2,1)S(1)}, bf16[512,128]{1,0:T(8,128)(2,1)}, u32[]{:S(2)}) copy-start(bf16[512,128]{1,0:T(8,128)(2,1)} %refs_17_.1) | copy-start | bytes 393220
  19.7 18.5 %copy-start.16 = (bf16[128,64]{0,1:T(8,128)(2,1)S(1)}, bf16[128,64]{0,1:T(8,128)(2,1)}, u32[]{:S(2)}) copy-start(bf16[128,64]{0,1:T(8,128)(2,1)} %param.35) | copy-start | bytes 49156
  22.7 9.0 %collective-permute-start.7 = (bf16[272,128]{1,0:T(8,128)(2,1)S(1)}, bf16[272,128]{1,0:T(8,128)(2,1)S(1)}, u32[]{:S(2)}, u32[]{:S(2)}) collective-permute-start(bf16[272,128]{1,0:T(8,128)(2,1)S(1)} %get-tuple-element.11.refs_0_), channel_id=1, source_target_pairs={{0,16},{1,24},{2,0},{3,8},{4,17},{5,25},{6,1},{7,9},{8,10},{9,2},{... | collective-permute-start | bytes 208904 | tf_op jit(solution)/shard_map/ppermute | solution.py:715
  23.6 8.1 %collective-permute-start.3 = (bf16[272,128]{1,0:T(8,128)(2,1)S(1)}, bf16[272,128]{1,0:T(8,128)(2,1)S(1)}, u32[]{:S(2)}, u32[]{:S(2)}) collective-permute-start(bf16[272,128]{1,0:T(8,128)(2,1)S(1)} %get-tuple-element.11.refs_0_), channel_id=1, source_target_pairs={{0,1},{1,0},{2,3},{3,2},{4,5},{5,4},{6,7},{7,6},{8,9},{9,8},{10,11... | collective-permute-start | bytes 208904 | tf_op jit(solution)/shard_map/ppermute | solution.py:718
  24.0 7.7 %collective-permute-start.2 = (bf16[272,128]{1,0:T(8,128)(2,1)S(1)}, bf16[272,128]{1,0:T(8,128)(2,1)S(1)}, u32[]{:S(2)}, u32[]{:S(2)}) collective-permute-start(bf16[272,128]{1,0:T(8,128)(2,1)S(1)} %get-tuple-element.11.refs_0_), channel_id=1, source_target_pairs={{0,6},{1,7},{2,4},{3,5},{4,2},{5,3},{6,0},{7,1},{8,14},{9,15},{10,... | collective-permute-start | bytes 208904 | tf_op jit(solution)/shard_map/ppermute | solution.py:718
  27.3 8.9 %collective-permute-start.1 = (bf16[272,128]{1,0:T(8,128)(2,1)S(1)}, bf16[272,128]{1,0:T(8,128)(2,1)S(1)}, u32[]{:S(2)}, u32[]{:S(2)}) collective-permute-start(bf16[272,128]{1,0:T(8,128)(2,1)S(1)} %get-tuple-element.11.refs_0_), channel_id=1, source_target_pairs={{0,4},{1,5},{2,6},{3,7},{4,0},{5,1},{6,2},{7,3},{8,12},{9,13},{10,... | collective-permute-start | bytes 208904 | tf_op jit(solution)/shard_map/ppermute | solution.py:718
  27.3 8.9 %collective-permute-start = (bf16[272,128]{1,0:T(8,128)(2,1)S(1)}, bf16[272,128]{1,0:T(8,128)(2,1)S(1)}, u32[]{:S(2)}, u32[]{:S(2)}) collective-permute-start(bf16[272,128]{1,0:T(8,128)(2,1)S(1)} %get-tuple-element.11.refs_0_), channel_id=1, source_target_pairs={{0,2},{1,3},{2,0},{3,1},{4,6},{5,7},{6,4},{7,5},{8,10},{9,11},{10,... | collective-permute-start | bytes 208904 | tf_op jit(solution)/shard_map/ppermute | solution.py:718
  31.7 5.3 %collective-permute-start.10 = (bf16[272,128]{1,0:T(8,128)(2,1)S(1)}, bf16[272,128]{1,0:T(8,128)(2,1)S(1)}, u32[]{:S(2)}, u32[]{:S(2)}) collective-permute-start(bf16[272,128]{1,0:T(8,128)(2,1)S(1)} %collective-permute-done.7.refs_8_), channel_id=1, source_target_pairs={{0,24},{8,16},{16,8},{24,0},{1,25},{9,17},{17,9},{25,1},{2,26},{10... | collective-permute-start | bytes 208904 | tf_op jit(solution)/shard_map/ppermute | solution.py:721
  31.7 6.2 %collective-permute-start.9 = (bf16[272,128]{1,0:T(8,128)(2,1)S(1)}, bf16[272,128]{1,0:T(8,128)(2,1)S(1)}, u32[]{:S(2)}, u32[]{:S(2)}) collective-permute-start(bf16[272,128]{1,0:T(8,128)(2,1)S(1)} %collective-permute-done.7.refs_8_), channel_id=1, source_target_pairs={{0,16},{8,24},{16,0},{24,8},{1,17},{9,25},{17,1},{25,9},{2,18},{10... | collective-permute-start | bytes 208904 | tf_op jit(solution)/shard_map/ppermute | solution.py:721
  31.7 6.2 %collective-permute-start.8 = (bf16[272,128]{1,0:T(8,128)(2,1)S(1)}, bf16[272,128]{1,0:T(8,128)(2,1)S(1)}, u32[]{:S(2)}, u32[]{:S(2)}) collective-permute-start(bf16[272,128]{1,0:T(8,128)(2,1)S(1)} %collective-permute-done.7.refs_8_), channel_id=1, source_target_pairs={{0,8},{8,0},{16,24},{24,16},{1,9},{9,1},{17,25},{25,17},{2,10},{10... | collective-permute-start | bytes 208904 | tf_op jit(solution)/shard_map/ppermute | solution.py:721
  36.2 1.7 %collective-permute-start.6 = (bf16[272,128]{1,0:T(8,128)(2,1)S(1)}, bf16[272,128]{1,0:T(8,128)(2,1)S(1)}, u32[]{:S(2)}, u32[]{:S(2)}) collective-permute-start(bf16[272,128]{1,0:T(8,128)(2,1)S(1)} %collective-permute-done.2.refs_3_), channel_id=1, source_target_pairs={{0,1},{1,0},{2,3},{3,2},{4,5},{5,4},{6,7},{7,6},{8,9},{9,8},{10,11... | collective-permute-start | bytes 208904 | tf_op jit(solution)/shard_map/ppermute | solution.py:718
  36.2 1.7 %collective-permute-start.5 = (bf16[272,128]{1,0:T(8,128)(2,1)S(1)}, bf16[272,128]{1,0:T(8,128)(2,1)S(1)}, u32[]{:S(2)}, u32[]{:S(2)}) collective-permute-start(bf16[272,128]{1,0:T(8,128)(2,1)S(1)} %collective-permute-done.1.refs_2_), channel_id=1, source_target_pairs={{0,1},{1,0},{2,3},{3,2},{4,5},{5,4},{6,7},{7,6},{8,9},{9,8},{10,11... | collective-permute-start | bytes 208904 | tf_op jit(solution)/shard_map/ppermute | solution.py:718
  37.0 1.3 %collective-permute-start.4 = (bf16[272,128]{1,0:T(8,128)(2,1)S(1)}, bf16[272,128]{1,0:T(8,128)(2,1)S(1)}, u32[]{:S(2)}, u32[]{:S(2)}) collective-permute-start(bf16[272,128]{1,0:T(8,128)(2,1)S(1)} %collective-permute-done.refs_1_), channel_id=1, source_target_pairs={{0,1},{1,0},{2,3},{3,2},{4,5},{5,4},{6,7},{7,6},{8,9},{9,8},{10,11... | collective-permute-start | bytes 208904 | tf_op jit(solution)/shard_map/ppermute | solution.py:718
  37.0 1.3 %copy-start = (bf16[1024,128]{1,0:T(8,128)(2,1)S(1)}, bf16[1024,128]{1,0:T(8,128)(2,1)}, u32[]{:S(2)}) copy-start(bf16[1024,128]{1,0:T(8,128)(2,1)} %turn.1._.refs_15_) | copy-start | bytes 786436
  37.0 1.3 %copy-start.1 = (bf16[1024,128]{1,0:T(8,128)(2,1)S(1)}, bf16[1024,128]{1,0:T(8,128)(2,1)}, u32[]{:S(2)}) copy-start(bf16[1024,128]{1,0:T(8,128)(2,1)} %get-tuple-element.9._2.refs_12_) | copy-start | bytes 786436

commit v3 on v2

--- a/solution.py
+++ b/solution.py
@@ -247,7 +247,7 @@
         if seqs & (seqs - 1) == 0:
             turned = (turned.astype(F32) * (1.0 / seqs)).astype(BF16)
         send_ref[seqs + t * LANES : seqs + (t + 1) * LANES, :] = turned
-    by_row = lax.broadcasted_iota(jnp.int32, (16, LANES), 0)
+    by_row = lax.broadcasted_iota(jnp.int32, (2 * n_res, LANES), 0)
     pairs = jnp.where(
         by_row < n_res, dot(amino_ref[...], re_ref[...]), dot(amino_ref[...], ce_ref[...])
     )
@@ -261,7 +261,7 @@
         functools.partial(attention_kernel, n_res),
         out_shape=(
             pltpu.VMEM((rows, feature), BF16),
-            pltpu.VMEM((2 * seqs + 16, LANES), BF16),
+            pltpu.VMEM((2 * (seqs + n_res), LANES), BF16),
         ),
         in_specs=[VMEM] * (2 + len(weights)) + [HBM] * len(ready),
         out_specs=(VMEM, VMEM),
@@ -465,17 +465,20 @@
     while todo:
         fill(todo.pop())
 
-    row_side = jnp.concatenate([r[2 * seqs : 2 * seqs + 16, :] for r in row_refs], axis=0)
-    col_side = jnp.concatenate([r[2 * seqs : 2 * seqs + 16, :] for r in col_refs], axis=0)
+    aux = 2 * n_res
+    side_r = jnp.concatenate([r[2 * seqs :, :].astype(F32) for r in row_refs], axis=0)
+    side_c = jnp.concatenate([r[2 * seqs :, :].astype(F32) for r in col_refs], axis=0)
+    row_side = side_r.astype(BF16)
+    col_side = side_c.astype(BF16)
 
     def pick(side, places, count):
         width = side.shape[0]
         line = lax.broadcasted_iota(jnp.int32, (count, width), 0)
         column = lax.broadcasted_iota(jnp.int32, (count, width), 1)
-        goal = column % 16 - n_res
+        goal = column % aux - n_res
         place = jnp.zeros_like(column)
         for slot, where in enumerate(places):
-            place = jnp.where(column // 16 == slot, where, place)
+            place = jnp.where(column // aux == slot, where, place)
         hit = (goal >= 0) & (goal < n_res) & (line == place * n_res + goal)
         return dot(jnp.where(hit, 1.0, 0.0).astype(BF16), side)
 
@@ -496,15 +499,13 @@
         project(1)
     else:
         for_chunks(total // chunk, project)
-    side_r = row_side.astype(F32)
-    side_c = col_side.astype(F32)
     place = 0
     for slot in range(n_row):
         for r in range(n_res):
             row = (r // PAIR * n_row + slot) * count_j
             lane = r % PAIR * LANES
             made = lhs_out[row : row + count_j, lane : lane + LANES]
-            left = side_r[slot * 16 + r : slot * 16 + r + 1, :]
+            left = side_r[slot * aux + r : slot * aux + r + 1, :]
             start[place : place + count_j, :] = (
                 (left + right_c) + rel_ref[place : place + count_j, :] + made
             )
@@ -514,7 +515,7 @@
             row = direct + (r // PAIR * n_col + slot) * count_i
             lane = r % PAIR * LANES
             made = lhs_out[row : row + count_i, lane : lane + LANES]
-            left = side_c[slot * 16 + r : slot * 16 + r + 1, :]
+            left = side_c[slot * aux + r : slot * aux + r + 1, :]
             start[place : place + count_i, :] = (
                 (left + right_r) + rel_ref[place : place + count_i, :] + made
             )
@@ -675,9 +676,7 @@
     grouped = latter_factor_matrix.reshape(feature, -1, GROUP)
     latter = jnp.einsum("pr,fge->pfgre", unit, grouped).reshape(n_res * feature, -1)
     factors = jnp.concatenate([jnp.kron(unit, former_factor_matrix), latter], axis=1)
-    amino_rows = jnp.concatenate(
-        [per_amino_features, per_amino_features, jnp.zeros((16 - 2 * n_res, feature), BF16)], axis=0
-    )
+    amino_rows = jnp.concatenate([per_amino_features, per_amino_features], axis=0)
     projection = turn_projection(factor_mean_projection)
     table = plane_offsets(n_rows, n_cols)
     inverse = []

time: 42.5 us -> 42.3 us (level)
  no operation moved by 1% of the time
where the time goes in v3:
time: 42.3 us; the launch traced here: 41.9 us
  starting transfers between devices  17 us (40%)
  Pallas kernels  10.6 us (25%)
  waiting for transfers between devices  10.2 us (24%)
  local copies, waits for them, and re-layouts  2.66 us (6%)
  between operations  0.95 us (2%)
    all_to_all x1, starting transfers between devices, shards(): moved = lax.all_to_all(sent, axes, split_axis=0, concat_axis=0, tiled=True)  7.33 us
    all_to_all x1, waiting for transfers between devices, shards(): moved = lax.all_to_all(sent, axes, split_axis=0, concat_axis=0, tiled=True)  5.51 us
    ppermute x7, starting transfers between devices, along_col(): return lax.ppermute(value, 'col', [(c, c ^ m) for c in range(n_cols)])  5.28 us
    pallas_call x1, Pallas kernels, pair_grid(): local_call(functools.partial(pair_kernel, n_row, n_col, n_res, seqs, plac...  3.8 us
    ppermute x3, starting transfers between devices, along_row(): return lax.ppermute(value, 'row', [(r, r ^ m) for r in range(n_rows)])  3.48 us
    ppermute x1, waiting for transfers between devices, shards(): turned = lax.ppermute(piece, axes, turn)  3.08 us
    pallas_call x1, Pallas kernels, attention(): local_call(functools.partial(attention_kernel, n_res), out_shape=(pltpu.V...  2.95 us
    pallas_call x1, Pallas kernels, chunks(): local_call(functools.partial(chunk_kernel, n_res, parts), out_shape=pltpu...  1.65 us
  transfers between devices with their start and end apart: 12, of which 5 were waited for; matrix products, arithmetic and copies ran while one was open for 4% of the time, Pallas kernels for 5%

profile of v3, /device:TPU:0, one launch (start us, length us, event | category | flops | bytes accessed | tf_op | source)
XLA Modules:
  0.0 41.9 jit_solution(5840549225262055222)
XLA Ops:
  0.6 1.7 %chunks.1 = bf16[512,256]{1,0:T(8,128)(2,1)} custom-call(bf16[4,128,256]{2,1,0:T(8,128)(2,1)} %x_far.1), custom_call_target="tpu_custom_call" | custom-call | tf_op jit(solution)/shard_map/chunks/pallas_call | solution.py:108
  2.3 0.0 copy-start.18
  2.3 7.3 %all-to-all-start = ((bf16[32,16,256]{2,1,0:T(8,128)(2,1)}), bf16[32,16,256]{2,1,0:T(8,128)(2,1)S(1)}, u32[]{:S(2)}, u32[]{:S(2)}) async-start(bf16[32,16,256]{2,1,0:T(8,128)(2,1)} %bitcast.23), calls=%async_computation | async-start | bytes 524288 | tf_op jit(solution)/shard_map/all_to_all | solution.py:672
  9.7 0.2 broadcast_multiply_fusion
  9.9 0.2 copy.25
  10.1 0.5 %copy-done.17 = bf16[256,32]{0,1:T(8,128)(2,1)S(1)} copy-done((bf16[256,32]{0,1:T(8,128)(2,1)S(1)}, bf16[256,32]{0,1:T(8,128)(2,1)}, u32[]{:S(2)}) %copy-start.17) | copy-done | bytes 16408
  10.6 0.2 broadcast_multiply_fusion.1
  10.8 0.0 copy-start.5
  10.8 0.0 copy-start.15
  10.9 0.0 copy-start.13
  10.9 0.0 copy-start.14
  10.9 0.2 copy.24
  11.1 0.7 %copy-done.5 = bf16[1024,128]{1,0:T(8,128)(2,1)S(1)} copy-done((bf16[1024,128]{1,0:T(8,128)(2,1)S(1)}, bf16[1024,128]{1,0:T(8,128)(2,1)}, u32[]{:S(2)}) %copy-start.5) | copy-done | bytes 262168
  11.8 1.0 %turn.1._.refs_15_ = bf16[1024,128]{1,0:T(8,128)(2,1)} custom-call(bf16[1024,128]{1,0:T(8,128)(2,1)S(1)} %copy-done.5), custom_call_target="tpu_custom_call" | custom-call | tf_op jit(solution)/shard_map/turn/pallas_call | solution.py:133
  12.8 1.2 %relative.1 = (bf16[1024,128]{1,0:T(8,128)(2,1)}, bf16[512,512]{1,0:T(8,128)(2,1)}) custom-call(bf16[65,128]{1,0:T(8,128)(2,1)S(1)} %copy-done.15), custom_call_target="tpu_custom_call" | custom-call | tf_op jit(solution)/shard_map/relative/pallas_call | solution.py:350
  14.1 0.1 pad_maximum_fusion.fg_ref
  14.1 5.5 %all-to-all-done = bf16[32,16,256]{2,1,0:T(8,128)(2,1)S(1)} async-done(((bf16[32,16,256]{2,1,0:T(8,128)(2,1)}), bf16[32,16,256]{2,1,0:T(8,128)(2,1)S(1)}, u32[]{:S(2)}, u32[]{:S(2)}) %all-to-all-start) | async-done | bytes 262176 | tf_op jit(solution)/shard_map/all_to_all | solution.py:672
  19.7 0.0 copy-start.11
  19.7 0.0 copy-start.12
  19.8 2.9 %attention.1 = (bf16[512,256]{1,0:T(8,128)(2,1)S(1)}, bf16[264,128]{1,0:T(8,128)(2,1)S(1)}) custom-call(bf16[512,256]{1,0:T(8,128)(2,1)S(1)} %bitcast.20, bf16[8,256]{1,0:T(8,128)(2,1)S(1)} %pad_maximum_fusion.1.amino_ref, bf16[256,256]{1,0:T(8,128)(2,1)S(1)} %copy-done.6, bf16[256,256]{1,0:T(8,128)(2,1)S(1)} %copy-done.7, bf16[256,256]{1,0:T(8,128)(2,1)S(1)} %copy-done.8, ...), custom_call_target="tpu_custom_call" | custom-call | tf_op jit(solution)/shard_map/attention/pallas_call | solution.py:260
  22.7 0.9 %collective-permute-start.7 = (bf16[264,128]{1,0:T(8,128)(2,1)S(1)}, bf16[264,128]{1,0:T(8,128)(2,1)S(1)}, u32[]{:S(2)}, u32[]{:S(2)}) collective-permute-start(bf16[264,128]{1,0:T(8,128)(2,1)S(1)} %get-tuple-element.11.refs_0_), channel_id=1, source_target_pairs={{0,16},{1,24},{2,0},{3,8},{4,17},{5,25},{6,1},{7,9},{8,10},{9,2},{... | collective-permute-start | bytes 202760 | tf_op jit(solution)/shard_map/ppermute | solution.py:714
  23.6 0.4 collective-permute-start.3
  24.0 3.3 %collective-permute-start.2 = (bf16[264,128]{1,0:T(8,128)(2,1)S(1)}, bf16[264,128]{1,0:T(8,128)(2,1)S(1)}, u32[]{:S(2)}, u32[]{:S(2)}) collective-permute-start(bf16[264,128]{1,0:T(8,128)(2,1)S(1)} %get-tuple-element.11.refs_0_), channel_id=1, source_target_pairs={{0,6},{1,7},{2,4},{3,5},{4,2},{5,3},{6,0},{7,1},{8,14},{9,15},{10,... | collective-permute-start | bytes 202760 | tf_op jit(solution)/shard_map/ppermute | solution.py:717
  27.3 1.1 %collective-permute-start = (bf16[264,128]{1,0:T(8,128)(2,1)S(1)}, bf16[264,128]{1,0:T(8,128)(2,1)S(1)}, u32[]{:S(2)}, u32[]{:S(2)}) collective-permute-start(bf16[264,128]{1,0:T(8,128)(2,1)S(1)} %get-tuple-element.11.refs_0_), channel_id=1, source_target_pairs={{0,2},{1,3},{2,0},{3,1},{4,6},{5,7},{6,4},{7,5},{8,10},{9,11},{10,... | collective-permute-start | bytes 202760 | tf_op jit(solution)/shard_map/ppermute | solution.py:717
  28.4 3.1 %collective-permute-done.7.refs_8_ = bf16[264,128]{1,0:T(8,128)(2,1)S(1)} collective-permute-done((bf16[264,128]{1,0:T(8,128)(2,1)S(1)}, bf16[264,128]{1,0:T(8,128)(2,1)S(1)}, u32[]{:S(2)}, u32[]{:S(2)}) %collective-permute-start.7) | collective-permute-done | bytes 67616 | tf_op jit(solution)/shard_map/ppermute | solution.py:714
  31.5 3.5 %collective-permute-start.8 = (bf16[264,128]{1,0:T(8,128)(2,1)S(1)}, bf16[264,128]{1,0:T(8,128)(2,1)S(1)}, u32[]{:S(2)}, u32[]{:S(2)}) collective-permute-start(bf16[264,128]{1,0:T(8,128)(2,1)S(1)} %collective-permute-done.7.refs_8_), channel_id=1, source_target_pairs={{0,8},{8,0},{16,24},{24,16},{1,9},{9,1},{17,25},{25,17},{2,10},{10... | collective-permute-start | bytes 202760 | tf_op jit(solution)/shard_map/ppermute | solution.py:720
  35.0 0.9 %collective-permute-done.1.refs_2_ = bf16[264,128]{1,0:T(8,128)(2,1)S(1)} collective-permute-done((bf16[264,128]{1,0:T(8,128)(2,1)S(1)}, bf16[264,128]{1,0:T(8,128)(2,1)S(1)}, u32[]{:S(2)}, u32[]{:S(2)}) %collective-permute-start.1) | collective-permute-done | bytes 67616 | tf_op jit(solution)/shard_map/ppermute | solution.py:717
  35.9 0.5 %collective-permute-start.5 = (bf16[264,128]{1,0:T(8,128)(2,1)S(1)}, bf16[264,128]{1,0:T(8,128)(2,1)S(1)}, u32[]{:S(2)}, u32[]{:S(2)}) collective-permute-start(bf16[264,128]{1,0:T(8,128)(2,1)S(1)} %collective-permute-done.1.refs_2_), channel_id=1, source_target_pairs={{0,1},{1,0},{2,3},{3,2},{4,5},{5,4},{6,7},{7,6},{8,9},{9,8},{10,11... | collective-permute-start | bytes 202760 | tf_op jit(solution)/shard_map/ppermute | solution.py:717
  36.4 0.3 collective-permute-done.10.refs_11_
  36.8 0.9 %copy.30 = bf16[4,128,256]{2,0,1:T(4,128)(2,1)} copy(bf16[4,128,256]{2,1,0:T(8,128)(2,1)S(1)} %bitcast.21) | data formatting | bytes 524288 | tf_op jit(solution)/shard_map/reshape | solution.py:708
  37.7 0.3 collective-permute-done.4.refs_5_
  38.1 3.8 %pairs.1 = (bf16[32,16,128]{2,1,0:T(8,128)(2,1)}, bf16[32,16,64]{2,1,0:T(8,128)(2,1)}) custom-call(bf16[264,128]{1,0:T(8,128)(2,1)S(1)} %get-tuple-element.11.refs_0_, bf16[264,128]{1,0:T(8,128)(2,1)S(1)} %collective-permute-done.refs_1_, bf16[264,128]{1,0:T(8,128)(2,1)S(1)} %collective-permute-done.1.refs_2_, ...), custom_call_target="tpu_custom_call" | custom-call | tf_op jit(solution)/shard_map/pairs/pallas_call | solution.py:599
  (48 shorter events, 0.2 us)
Async XLA Ops:
  2.3 7.4 %copy-start.18 = (bf16[256,32]{0,1:T(8,128)(2,1)S(1)}, bf16[256,32]{0,1:T(8,128)(2,1)}, u32[]{:S(2)}) copy-start(bf16[256,32]{0,1:T(8,128)(2,1)} %param.28) | copy-start | bytes 49156
  2.3 17.3 %all-to-all-start = ((bf16[32,16,256]{2,1,0:T(8,128)(2,1)}), bf16[32,16,256]{2,1,0:T(8,128)(2,1)S(1)}, u32[]{:S(2)}, u32[]{:S(2)}) async-start(bf16[32,16,256]{2,1,0:T(8,128)(2,1)} %bitcast.23), calls=%async_computation | async-start | bytes 524288 | tf_op jit(solution)/shard_map/all_to_all | solution.py:672
  9.9 0.7 %copy-start.17 = (bf16[256,32]{0,1:T(8,128)(2,1)S(1)}, bf16[256,32]{0,1:T(8,128)(2,1)}, u32[]{:S(2)}) copy-start(bf16[256,32]{0,1:T(8,128)(2,1)} %param.27) | copy-start | bytes 49156
  10.8 1.0 %copy-start.5 = (bf16[1024,128]{1,0:T(8,128)(2,1)S(1)}, bf16[1024,128]{1,0:T(8,128)(2,1)}, u32[]{:S(2)}) copy-start(bf16[1024,128]{1,0:T(8,128)(2,1)} %w_ref.1) | copy-start | bytes 786436
  10.8 2.0 %copy-start.15 = (bf16[65,128]{1,0:T(8,128)(2,1)S(1)}, bf16[65,128]{1,0:T(8,128)(2,1)}, u32[]{:S(2)}) copy-start(bf16[65,128]{1,0:T(8,128)(2,1)} %off_ref.1) | copy-start | bytes 49924
  10.8 3.2 %copy-start.19 = (bf16[4,256]{1,0:T(4,128)(2,1)S(1)}, bf16[4,256]{1,0:T(4,128)(2,1)}, u32[]{:S(2)}) copy-start(bf16[4,256]{1,0:T(4,128)(2,1)} %param.19) | copy-start | bytes 6148
  10.8 8.8 %copy-start.10 = (bf16[256,256]{1,0:T(8,128)(2,1)S(1)}, bf16[256,256]{1,0:T(8,128)(2,1)}, u32[]{:S(2)}) copy-start(bf16[256,256]{1,0:T(8,128)(2,1)} %wo_ref.1) | copy-start | bytes 393220
  10.9 8.8 %copy-start.13 = (bf16[256,128]{1,0:T(8,128)(2,1)S(1)}, bf16[256,128]{1,0:T(8,128)(2,1)}, u32[]{:S(2)}) copy-start(bf16[256,128]{1,0:T(8,128)(2,1)} %re_ref.1) | copy-start | bytes 196612
  10.9 8.8 %copy-start.14 = (bf16[256,128]{1,0:T(8,128)(2,1)S(1)}, bf16[256,128]{1,0:T(8,128)(2,1)}, u32[]{:S(2)}) copy-start(bf16[256,128]{1,0:T(8,128)(2,1)} %ce_ref.1) | copy-start | bytes 196612
  11.8 7.9 %copy-start.6 = (bf16[256,256]{1,0:T(8,128)(2,1)S(1)}, bf16[256,256]{1,0:T(8,128)(2,1)}, u32[]{:S(2)}) copy-start(bf16[256,256]{1,0:T(8,128)(2,1)} %wq_ref.1) | copy-start | bytes 393220
  11.8 7.9 %copy-start.7 = (bf16[256,256]{1,0:T(8,128)(2,1)S(1)}, bf16[256,256]{1,0:T(8,128)(2,1)}, u32[]{:S(2)}) copy-start(bf16[256,256]{1,0:T(8,128)(2,1)} %wk_ref.1) | copy-start | bytes 393220
  11.8 7.9 %copy-start.8 = (bf16[256,256]{1,0:T(8,128)(2,1)S(1)}, bf16[256,256]{1,0:T(8,128)(2,1)}, u32[]{:S(2)}) copy-start(bf16[256,256]{1,0:T(8,128)(2,1)} %wv_ref.1) | copy-start | bytes 393220
  11.8 7.9 %copy-start.9 = (bf16[256,256]{1,0:T(8,128)(2,1)S(1)}, bf16[256,256]{1,0:T(8,128)(2,1)}, u32[]{:S(2)}) copy-start(bf16[256,256]{1,0:T(8,128)(2,1)} %wg_ref.1) | copy-start | bytes 393220
  14.0 5.7 %copy-start.2 = (bf16[256,1024]{1,0:T(8,128)(2,1)S(1)}, bf16[256,1024]{1,0:T(8,128)(2,1)}, u32[]{:S(2)}) copy-start(bf16[256,1024]{1,0:T(8,128)(2,1)} %w1_ref.1) | copy-start | bytes 1572868
  14.0 5.7 %copy-start.3 = (bf16[1024,256]{1,0:T(8,128)(2,1)S(1)}, bf16[1024,256]{1,0:T(8,128)(2,1)}, u32[]{:S(2)}) copy-start(bf16[1024,256]{1,0:T(8,128)(2,1)} %w2_ref.1) | copy-start | bytes 1572868
  19.7 18.3 %copy-start.4 = (bf16[512,512]{1,0:T(8,128)(2,1)S(1)}, bf16[512,512]{1,0:T(8,128)(2,1)}, u32[]{:S(2)}) copy-start(bf16[512,512]{1,0:T(8,128)(2,1)} %get-tuple-element.12.refs_13_) | copy-start | bytes 1572868
  19.7 18.3 %copy-start.11 = (bf16[128,512]{1,0:T(8,128)(2,1)S(1)}, bf16[128,512]{1,0:T(8,128)(2,1)}, u32[]{:S(2)}) copy-start(bf16[128,512]{1,0:T(8,128)(2,1)} %refs_16_.1) | copy-start | bytes 393220
  19.7 18.3 %copy-start.12 = (bf16[512,128]{1,0:T(8,128)(2,1)S(1)}, bf16[512,128]{1,0:T(8,128)(2,1)}, u32[]{:S(2)}) copy-start(bf16[512,128]{1,0:T(8,128)(2,1)} %refs_17_.1) | copy-start | bytes 393220
  19.7 18.3 %copy-start.16 = (bf16[128,64]{0,1:T(8,128)(2,1)S(1)}, bf16[128,64]{0,1:T(8,128)(2,1)}, u32[]{:S(2)}) copy-start(bf16[128,64]{0,1:T(8,128)(2,1)} %param.35) | copy-start | bytes 49156
  22.7 8.8 %collective-permute-start.7 = (bf16[264,128]{1,0:T(8,128)(2,1)S(1)}, bf16[264,128]{1,0:T(8,128)(2,1)S(1)}, u32[]{:S(2)}, u32[]{:S(2)}) collective-permute-start(bf16[264,128]{1,0:T(8,128)(2,1)S(1)} %get-tuple-element.11.refs_0_), channel_id=1, source_target_pairs={{0,16},{1,24},{2,0},{3,8},{4,17},{5,25},{6,1},{7,9},{8,10},{9,2},{... | collective-permute-start | bytes 202760 | tf_op jit(solution)/shard_map/ppermute | solution.py:714
  23.6 7.9 %collective-permute-start.3 = (bf16[264,128]{1,0:T(8,128)(2,1)S(1)}, bf16[264,128]{1,0:T(8,128)(2,1)S(1)}, u32[]{:S(2)}, u32[]{:S(2)}) collective-permute-start(bf16[264,128]{1,0:T(8,128)(2,1)S(1)} %get-tuple-element.11.refs_0_), channel_id=1, source_target_pairs={{0,1},{1,0},{2,3},{3,2},{4,5},{5,4},{6,7},{7,6},{8,9},{9,8},{10,11... | collective-permute-start | bytes 202760 | tf_op jit(solution)/shard_map/ppermute | solution.py:717
  24.0 7.5 %collective-permute-start.2 = (bf16[264,128]{1,0:T(8,128)(2,1)S(1)}, bf16[264,128]{1,0:T(8,128)(2,1)S(1)}, u32[]{:S(2)}, u32[]{:S(2)}) collective-permute-start(bf16[264,128]{1,0:T(8,128)(2,1)S(1)} %get-tuple-element.11.refs_0_), channel_id=1, source_target_pairs={{0,6},{1,7},{2,4},{3,5},{4,2},{5,3},{6,0},{7,1},{8,14},{9,15},{10,... | collective-permute-start | bytes 202760 | tf_op jit(solution)/shard_map/ppermute | solution.py:717
  27.3 8.6 %collective-permute-start.1 = (bf16[264,128]{1,0:T(8,128)(2,1)S(1)}, bf16[264,128]{1,0:T(8,128)(2,1)S(1)}, u32[]{:S(2)}, u32[]{:S(2)}) collective-permute-start(bf16[264,128]{1,0:T(8,128)(2,1)S(1)} %get-tuple-element.11.refs_0_), channel_id=1, source_target_pairs={{0,4},{1,5},{2,6},{3,7},{4,0},{5,1},{6,2},{7,3},{8,12},{9,13},{10,... | collective-permute-start | bytes 202760 | tf_op jit(solution)/shard_map/ppermute | solution.py:717
  27.3 8.6 %collective-permute-start = (bf16[264,128]{1,0:T(8,128)(2,1)S(1)}, bf16[264,128]{1,0:T(8,128)(2,1)S(1)}, u32[]{:S(2)}, u32[]{:S(2)}) collective-permute-start(bf16[264,128]{1,0:T(8,128)(2,1)S(1)} %get-tuple-element.11.refs_0_), channel_id=1, source_target_pairs={{0,2},{1,3},{2,0},{3,1},{4,6},{5,7},{6,4},{7,5},{8,10},{9,11},{10,... | collective-permute-start | bytes 202760 | tf_op jit(solution)/shard_map/ppermute | solution.py:717
  31.5 5.3 %collective-permute-start.10 = (bf16[264,128]{1,0:T(8,128)(2,1)S(1)}, bf16[264,128]{1,0:T(8,128)(2,1)S(1)}, u32[]{:S(2)}, u32[]{:S(2)}) collective-permute-start(bf16[264,128]{1,0:T(8,128)(2,1)S(1)} %collective-permute-done.7.refs_8_), channel_id=1, source_target_pairs={{0,24},{8,16},{16,8},{24,0},{1,25},{9,17},{17,9},{25,1},{2,26},{10... | collective-permute-start | bytes 202760 | tf_op jit(solution)/shard_map/ppermute | solution.py:720
  31.5 6.2 %collective-permute-start.9 = (bf16[264,128]{1,0:T(8,128)(2,1)S(1)}, bf16[264,128]{1,0:T(8,128)(2,1)S(1)}, u32[]{:S(2)}, u32[]{:S(2)}) collective-permute-start(bf16[264,128]{1,0:T(8,128)(2,1)S(1)} %collective-permute-done.7.refs_8_), channel_id=1, source_target_pairs={{0,16},{8,24},{16,0},{24,8},{1,17},{9,25},{17,1},{25,9},{2,18},{10... | collective-permute-start | bytes 202760 | tf_op jit(solution)/shard_map/ppermute | solution.py:720
  31.5 6.2 %collective-permute-start.8 = (bf16[264,128]{1,0:T(8,128)(2,1)S(1)}, bf16[264,128]{1,0:T(8,128)(2,1)S(1)}, u32[]{:S(2)}, u32[]{:S(2)}) collective-permute-start(bf16[264,128]{1,0:T(8,128)(2,1)S(1)} %collective-permute-done.7.refs_8_), channel_id=1, source_target_pairs={{0,8},{8,0},{16,24},{24,16},{1,9},{9,1},{17,25},{25,17},{2,10},{10... | collective-permute-start | bytes 202760 | tf_op jit(solution)/shard_map/ppermute | solution.py:720
  35.9 1.8 %collective-permute-start.6 = (bf16[264,128]{1,0:T(8,128)(2,1)S(1)}, bf16[264,128]{1,0:T(8,128)(2,1)S(1)}, u32[]{:S(2)}, u32[]{:S(2)}) collective-permute-start(bf16[264,128]{1,0:T(8,128)(2,1)S(1)} %collective-permute-done.2.refs_3_), channel_id=1, source_target_pairs={{0,1},{1,0},{2,3},{3,2},{4,5},{5,4},{6,7},{7,6},{8,9},{9,8},{10,11... | collective-permute-start | bytes 202760 | tf_op jit(solution)/shard_map/ppermute | solution.py:717
  35.9 1.8 %collective-permute-start.5 = (bf16[264,128]{1,0:T(8,128)(2,1)S(1)}, bf16[264,128]{1,0:T(8,128)(2,1)S(1)}, u32[]{:S(2)}, u32[]{:S(2)}) collective-permute-start(bf16[264,128]{1,0:T(8,128)(2,1)S(1)} %collective-permute-done.1.refs_2_), channel_id=1, source_target_pairs={{0,1},{1,0},{2,3},{3,2},{4,5},{5,4},{6,7},{7,6},{8,9},{9,8},{10,11... | collective-permute-start | bytes 202760 | tf_op jit(solution)/shard_map/ppermute | solution.py:717
  36.8 1.3 %collective-permute-start.4 = (bf16[264,128]{1,0:T(8,128)(2,1)S(1)}, bf16[264,128]{1,0:T(8,128)(2,1)S(1)}, u32[]{:S(2)}, u32[]{:S(2)}) collective-permute-start(bf16[264,128]{1,0:T(8,128)(2,1)S(1)} %collective-permute-done.refs_1_), channel_id=1, source_target_pairs={{0,1},{1,0},{2,3},{3,2},{4,5},{5,4},{6,7},{7,6},{8,9},{9,8},{10,11... | collective-permute-start | bytes 202760 | tf_op jit(solution)/shard_map/ppermute | solution.py:717
  36.8 1.3 %copy-start = (bf16[1024,128]{1,0:T(8,128)(2,1)S(1)}, bf16[1024,128]{1,0:T(8,128)(2,1)}, u32[]{:S(2)}) copy-start(bf16[1024,128]{1,0:T(8,128)(2,1)} %turn.1._.refs_15_) | copy-start | bytes 786436
  36.8 1.3 %copy-start.1 = (bf16[1024,128]{1,0:T(8,128)(2,1)S(1)}, bf16[1024,128]{1,0:T(8,128)(2,1)}, u32[]{:S(2)}) copy-start(bf16[1024,128]{1,0:T(8,128)(2,1)} %get-tuple-element.9._2.refs_12_) | copy-start | bytes 786436

commit v4 on v3

--- a/solution.py
+++ b/solution.py
@@ -631,7 +631,7 @@
         home = column // 2
         far = sorted(
             range(n_row),
-            key=lambda m: (-abs((column * n_row + m) % n_col // 2 - home), m),
+            key=lambda m: (-abs((column * n_row + m) % n_col // 2 - home), -m),
         )
         line = [0] * n_row
         for position, m in enumerate(far):
@@ -720,7 +720,9 @@
         return lax.ppermute(value, "row", [(r, r ^ m) for r in range(n_rows)])
 
 
-    own = [piece] + [along_col(piece, 2 * m) for m in range(1, n_cols // 2)]
+    own = [piece]
+    for m in range(1, n_cols // 2):
+        own.append(along_col(piece, 2 * m))
     other = [along_col(value, 1) for value in own[1:]]
     other = [along_col(piece, 1)] + other
     col_pieces = [turned] + [along_row(turned, m) for m in range(1, n_rows)]

time: 42.3 us -> 42.5 us (level)
    ppermute x7, waiting for transfers between devices: 1.27 us -> 4.85 us  [along_col(): return lax.ppermute(value, 'col', [(c, c ^ m) for c in range(n_cols)])]
    ppermute x1, waiting for transfers between devices: 3.08 us -> 0.01 us  [shards(): turned = lax.ppermute(piece, axes, turn)]
    ppermute x3, starting transfers between devices: 3.48 us -> 2.84 us  [along_row(): return lax.ppermute(value, 'row', [(r, r ^ m) for r in range(n_rows)])]
  transfers between devices with their start and end apart: 12 -> 12, of which waited for: 5 -> 3; matrix products, arithmetic and copies ran while one was open for 4% -> 4% of each run, Pallas kernels for 5% -> 5%
where the time goes in v4:
time: 42.5 us; the launch traced here: 42.1 us
  starting transfers between devices  17 us (40%)
  Pallas kernels  10.6 us (25%)
  waiting for transfers between devices  10.4 us (24%)
  local copies, waits for them, and re-layouts  2.69 us (6%)
  between operations  0.96 us (2%)
    all_to_all x1, starting transfers between devices, shards(): moved = lax.all_to_all(sent, axes, split_axis=0, concat_axis=0, tiled=True)  7.33 us
    ppermute x7, starting transfers between devices, along_col(): return lax.ppermute(value, 'col', [(c, c ^ m) for c in range(n_cols)])  5.66 us
    all_to_all x1, waiting for transfers between devices, shards(): moved = lax.all_to_all(sent, axes, split_axis=0, concat_axis=0, tiled=True)  5.51 us
    ppermute x7, waiting for transfers between devices, along_col(): return lax.ppermute(value, 'col', [(c, c ^ m) for c in range(n_cols)])  4.85 us
    pallas_call x1, Pallas kernels, pair_grid(): local_call(functools.partial(pair_kernel, n_row, n_col, n_res, seqs, plac...  3.79 us
    pallas_call x1, Pallas kernels, attention(): local_call(functools.partial(attention_kernel, n_res), out_shape=(pltpu.V...  2.95 us
    ppermute x3, starting transfers between devices, along_row(): return lax.ppermute(value, 'row', [(r, r ^ m) for r in range(n_rows)])  2.84 us
    pallas_call x1, Pallas kernels, chunks(): local_call(functools.partial(chunk_kernel, n_res, parts), out_shape=pltpu...  1.65 us
  transfers between devices with their start and end apart: 12, of which 3 were waited for; matrix products, arithmetic and copies ran while one was open for 4% of the time, Pallas kernels for 5%

profile of v4, /device:TPU:0, one launch (start us, length us, event | category | flops | bytes accessed | tf_op | source)
XLA Modules:
  0.0 42.1 jit_solution(10169875540128391476)
XLA Ops:
  0.6 1.7 %chunks.1 = bf16[512,256]{1,0:T(8,128)(2,1)} custom-call(bf16[4,128,256]{2,1,0:T(8,128)(2,1)} %x_far.1), custom_call_target="tpu_custom_call" | custom-call | tf_op jit(solution)/shard_map/chunks/pallas_call | solution.py:108
  2.3 7.3 %all-to-all-start = ((bf16[32,16,256]{2,1,0:T(8,128)(2,1)}), bf16[32,16,256]{2,1,0:T(8,128)(2,1)S(1)}, u32[]{:S(2)}, u32[]{:S(2)}) async-start(bf16[32,16,256]{2,1,0:T(8,128)(2,1)} %bitcast.23), calls=%async_computation | async-start | bytes 524288 | tf_op jit(solution)/shard_map/all_to_all | solution.py:672
  9.7 0.2 broadcast_multiply_fusion
  9.9 0.2 copy.25
  10.1 0.5 %copy-done.17 = bf16[256,32]{0,1:T(8,128)(2,1)S(1)} copy-done((bf16[256,32]{0,1:T(8,128)(2,1)S(1)}, bf16[256,32]{0,1:T(8,128)(2,1)}, u32[]{:S(2)}) %copy-start.17) | copy-done | bytes 16408
  10.6 0.2 broadcast_multiply_fusion.1
  10.8 0.0 copy-start.5
  10.8 0.0 copy-start.15
  10.9 0.0 copy-start.13
  10.9 0.0 copy-start.14
  10.9 0.2 copy.24
  11.1 0.7 %copy-done.5 = bf16[1024,128]{1,0:T(8,128)(2,1)S(1)} copy-done((bf16[1024,128]{1,0:T(8,128)(2,1)S(1)}, bf16[1024,128]{1,0:T(8,128)(2,1)}, u32[]{:S(2)}) %copy-start.5) | copy-done | bytes 262168
  11.8 1.0 %turn.1._.refs_15_ = bf16[1024,128]{1,0:T(8,128)(2,1)} custom-call(bf16[1024,128]{1,0:T(8,128)(2,1)S(1)} %copy-done.5), custom_call_target="tpu_custom_call" | custom-call | tf_op jit(solution)/shard_map/turn/pallas_call | solution.py:133
  12.8 1.2 %relative.1 = (bf16[1024,128]{1,0:T(8,128)(2,1)}, bf16[512,512]{1,0:T(8,128)(2,1)}) custom-call(bf16[65,128]{1,0:T(8,128)(2,1)S(1)} %copy-done.15), custom_call_target="tpu_custom_call" | custom-call | tf_op jit(solution)/shard_map/relative/pallas_call | solution.py:350
  14.1 0.1 pad_maximum_fusion.fg_ref
  14.1 5.5 %all-to-all-done = bf16[32,16,256]{2,1,0:T(8,128)(2,1)S(1)} async-done(((bf16[32,16,256]{2,1,0:T(8,128)(2,1)}), bf16[32,16,256]{2,1,0:T(8,128)(2,1)S(1)}, u32[]{:S(2)}, u32[]{:S(2)}) %all-to-all-start) | async-done | bytes 262176 | tf_op jit(solution)/shard_map/all_to_all | solution.py:672
  19.7 0.0 copy-start.11
  19.7 0.0 copy-start.12
  19.8 2.9 %attention.1 = (bf16[512,256]{1,0:T(8,128)(2,1)S(1)}, bf16[264,128]{1,0:T(8,128)(2,1)S(1)}) custom-call(bf16[512,256]{1,0:T(8,128)(2,1)S(1)} %bitcast.20, bf16[8,256]{1,0:T(8,128)(2,1)S(1)} %pad_maximum_fusion.1.amino_ref, bf16[256,256]{1,0:T(8,128)(2,1)S(1)} %copy-done.6, bf16[256,256]{1,0:T(8,128)(2,1)S(1)} %copy-done.7, bf16[256,256]{1,0:T(8,128)(2,1)S(1)} %copy-done.8, ...), custom_call_target="tpu_custom_call" | custom-call | tf_op jit(solution)/shard_map/attention/pallas_call | solution.py:260
  22.7 1.2 %collective-permute-start.7 = (bf16[264,128]{1,0:T(8,128)(2,1)S(1)}, bf16[264,128]{1,0:T(8,128)(2,1)S(1)}, u32[]{:S(2)}, u32[]{:S(2)}) collective-permute-start(bf16[264,128]{1,0:T(8,128)(2,1)S(1)} %get-tuple-element.11.refs_0_), channel_id=1, source_target_pairs={{0,24},{1,16},{2,8},{3,0},{4,25},{5,17},{6,9},{7,1},{8,2},{9,10},{... | collective-permute-start | bytes 202760 | tf_op jit(solution)/shard_map/ppermute | solution.py:714
  23.9 3.3 %collective-permute-start.2 = (bf16[264,128]{1,0:T(8,128)(2,1)S(1)}, bf16[264,128]{1,0:T(8,128)(2,1)S(1)}, u32[]{:S(2)}, u32[]{:S(2)}) collective-permute-start(bf16[264,128]{1,0:T(8,128)(2,1)S(1)} %get-tuple-element.11.refs_0_), channel_id=1, source_target_pairs={{0,6},{1,7},{2,4},{3,5},{4,2},{5,3},{6,0},{7,1},{8,14},{9,15},{10,... | collective-permute-start | bytes 202760 | tf_op jit(solution)/shard_map/ppermute | solution.py:717
  27.2 1.1 %collective-permute-start = (bf16[264,128]{1,0:T(8,128)(2,1)S(1)}, bf16[264,128]{1,0:T(8,128)(2,1)S(1)}, u32[]{:S(2)}, u32[]{:S(2)}) collective-permute-start(bf16[264,128]{1,0:T(8,128)(2,1)S(1)} %get-tuple-element.11.refs_0_), channel_id=1, source_target_pairs={{0,2},{1,3},{2,0},{3,1},{4,6},{5,7},{6,4},{7,5},{8,10},{9,11},{10,... | collective-permute-start | bytes 202760 | tf_op jit(solution)/shard_map/ppermute | solution.py:717
  28.3 2.0 %collective-permute-start.10 = (bf16[264,128]{1,0:T(8,128)(2,1)S(1)}, bf16[264,128]{1,0:T(8,128)(2,1)S(1)}, u32[]{:S(2)}, u32[]{:S(2)}) collective-permute-start(bf16[264,128]{1,0:T(8,128)(2,1)S(1)} %collective-permute-done.7.refs_8_), channel_id=1, source_target_pairs={{0,24},{8,16},{16,8},{24,0},{1,25},{9,17},{17,9},{25,1},{2,26},{10... | collective-permute-start | bytes 202760 | tf_op jit(solution)/shard_map/ppermute | solution.py:720
  30.4 0.5 %collective-permute-start.9 = (bf16[264,128]{1,0:T(8,128)(2,1)S(1)}, bf16[264,128]{1,0:T(8,128)(2,1)S(1)}, u32[]{:S(2)}, u32[]{:S(2)}) collective-permute-start(bf16[264,128]{1,0:T(8,128)(2,1)S(1)} %collective-permute-done.7.refs_8_), channel_id=1, source_target_pairs={{0,16},{8,24},{16,0},{24,8},{1,17},{9,25},{17,1},{25,9},{2,18},{10... | collective-permute-start | bytes 202760 | tf_op jit(solution)/shard_map/ppermute | solution.py:720
  30.8 0.7 %collective-permute-done.2.refs_3_ = bf16[264,128]{1,0:T(8,128)(2,1)S(1)} collective-permute-done((bf16[264,128]{1,0:T(8,128)(2,1)S(1)}, bf16[264,128]{1,0:T(8,128)(2,1)S(1)}, u32[]{:S(2)}, u32[]{:S(2)}) %collective-permute-start.2) | collective-permute-done | bytes 67616 | tf_op jit(solution)/shard_map/ppermute | solution.py:717
  31.6 0.3 collective-permute-start.8
  31.9 4.1 %collective-permute-done.1.refs_2_ = bf16[264,128]{1,0:T(8,128)(2,1)S(1)} collective-permute-done((bf16[264,128]{1,0:T(8,128)(2,1)S(1)}, bf16[264,128]{1,0:T(8,128)(2,1)S(1)}, u32[]{:S(2)}, u32[]{:S(2)}) %collective-permute-start.1) | collective-permute-done | bytes 67616 | tf_op jit(solution)/shard_map/ppermute | solution.py:717
  36.0 0.5 %collective-permute-start.5 = (bf16[264,128]{1,0:T(8,128)(2,1)S(1)}, bf16[264,128]{1,0:T(8,128)(2,1)S(1)}, u32[]{:S(2)}, u32[]{:S(2)}) collective-permute-start(bf16[264,128]{1,0:T(8,128)(2,1)S(1)} %collective-permute-done.1.refs_2_), channel_id=1, source_target_pairs={{0,1},{1,0},{2,3},{3,2},{4,5},{5,4},{6,7},{7,6},{8,9},{9,8},{10,11... | collective-permute-start | bytes 202760 | tf_op jit(solution)/shard_map/ppermute | solution.py:717
  36.5 0.8 %collective-permute-start.4 = (bf16[264,128]{1,0:T(8,128)(2,1)S(1)}, bf16[264,128]{1,0:T(8,128)(2,1)S(1)}, u32[]{:S(2)}, u32[]{:S(2)}) collective-permute-start(bf16[264,128]{1,0:T(8,128)(2,1)S(1)} %collective-permute-done.refs_1_), channel_id=1, source_target_pairs={{0,1},{1,0},{2,3},{3,2},{4,5},{5,4},{6,7},{7,6},{8,9},{9,8},{10,11... | collective-permute-start | bytes 202760 | tf_op jit(solution)/shard_map/ppermute | solution.py:717
  37.3 0.9 %copy.30 = bf16[4,128,256]{2,0,1:T(4,128)(2,1)} copy(bf16[4,128,256]{2,1,0:T(8,128)(2,1)S(1)} %bitcast.21) | data formatting | bytes 524288 | tf_op jit(solution)/shard_map/reshape | solution.py:708
  38.3 0.0 copy-done.1
  38.3 3.8 %pairs.1 = (bf16[32,16,128]{2,1,0:T(8,128)(2,1)}, bf16[32,16,64]{2,1,0:T(8,128)(2,1)}) custom-call(bf16[264,128]{1,0:T(8,128)(2,1)S(1)} %get-tuple-element.11.refs_0_, bf16[264,128]{1,0:T(8,128)(2,1)S(1)} %collective-permute-done.refs_1_, bf16[264,128]{1,0:T(8,128)(2,1)S(1)} %collective-permute-done.1.refs_2_, ...), custom_call_target="tpu_custom_call" | custom-call | tf_op jit(solution)/shard_map/pairs/pallas_call | solution.py:599
  (48 shorter events, 0.2 us)
Async XLA Ops:
  2.3 7.4 %copy-start.18 = (bf16[256,32]{0,1:T(8,128)(2,1)S(1)}, bf16[256,32]{0,1:T(8,128)(2,1)}, u32[]{:S(2)}) copy-start(bf16[256,32]{0,1:T(8,128)(2,1)} %param.28) | copy-start | bytes 49156
  2.3 17.3 %all-to-all-start = ((bf16[32,16,256]{2,1,0:T(8,128)(2,1)}), bf16[32,16,256]{2,1,0:T(8,128)(2,1)S(1)}, u32[]{:S(2)}, u32[]{:S(2)}) async-start(bf16[32,16,256]{2,1,0:T(8,128)(2,1)} %bitcast.23), calls=%async_computation | async-start | bytes 524288 | tf_op jit(solution)/shard_map/all_to_all | solution.py:672
  9.9 0.7 %copy-start.17 = (bf16[256,32]{0,1:T(8,128)(2,1)S(1)}, bf16[256,32]{0,1:T(8,128)(2,1)}, u32[]{:S(2)}) copy-start(bf16[256,32]{0,1:T(8,128)(2,1)} %param.27) | copy-start | bytes 49156
  10.8 1.0 %copy-start.5 = (bf16[1024,128]{1,0:T(8,128)(2,1)S(1)}, bf16[1024,128]{1,0:T(8,128)(2,1)}, u32[]{:S(2)}) copy-start(bf16[1024,128]{1,0:T(8,128)(2,1)} %w_ref.1) | copy-start | bytes 786436
  10.8 2.0 %copy-start.15 = (bf16[65,128]{1,0:T(8,128)(2,1)S(1)}, bf16[65,128]{1,0:T(8,128)(2,1)}, u32[]{:S(2)}) copy-start(bf16[65,128]{1,0:T(8,128)(2,1)} %off_ref.1) | copy-start | bytes 49924
  10.8 3.2 %copy-start.19 = (bf16[4,256]{1,0:T(4,128)(2,1)S(1)}, bf16[4,256]{1,0:T(4,128)(2,1)}, u32[]{:S(2)}) copy-start(bf16[4,256]{1,0:T(4,128)(2,1)} %param.19) | copy-start | bytes 6148
  10.8 8.8 %copy-start.10 = (bf16[256,256]{1,0:T(8,128)(2,1)S(1)}, bf16[256,256]{1,0:T(8,128)(2,1)}, u32[]{:S(2)}) copy-start(bf16[256,256]{1,0:T(8,128)(2,1)} %wo_ref.1) | copy-start | bytes 393220
  10.9 8.8 %copy-start.13 = (bf16[256,128]{1,0:T(8,128)(2,1)S(1)}, bf16[256,128]{1,0:T(8,128)(2,1)}, u32[]{:S(2)}) copy-start(bf16[256,128]{1,0:T(8,128)(2,1)} %re_ref.1) | copy-start | bytes 196612
  10.9 8.8 %copy-start.14 = (bf16[256,128]{1,0:T(8,128)(2,1)S(1)}, bf16[256,128]{1,0:T(8,128)(2,1)}, u32[]{:S(2)}) copy-start(bf16[256,128]{1,0:T(8,128)(2,1)} %ce_ref.1) | copy-start | bytes 196612
  11.8 7.9 %copy-start.6 = (bf16[256,256]{1,0:T(8,128)(2,1)S(1)}, bf16[256,256]{1,0:T(8,128)(2,1)}, u32[]{:S(2)}) copy-start(bf16[256,256]{1,0:T(8,128)(2,1)} %wq_ref.1) | copy-start | bytes 393220
  11.8 7.9 %copy-start.7 = (bf16[256,256]{1,0:T(8,128)(2,1)S(1)}, bf16[256,256]{1,0:T(8,128)(2,1)}, u32[]{:S(2)}) copy-start(bf16[256,256]{1,0:T(8,128)(2,1)} %wk_ref.1) | copy-start | bytes 393220
  11.8 7.9 %copy-start.8 = (bf16[256,256]{1,0:T(8,128)(2,1)S(1)}, bf16[256,256]{1,0:T(8,128)(2,1)}, u32[]{:S(2)}) copy-start(bf16[256,256]{1,0:T(8,128)(2,1)} %wv_ref.1) | copy-start | bytes 393220
  11.8 7.9 %copy-start.9 = (bf16[256,256]{1,0:T(8,128)(2,1)S(1)}, bf16[256,256]{1,0:T(8,128)(2,1)}, u32[]{:S(2)}) copy-start(bf16[256,256]{1,0:T(8,128)(2,1)} %wg_ref.1) | copy-start | bytes 393220
  14.0 5.7 %copy-start.2 = (bf16[256,1024]{1,0:T(8,128)(2,1)S(1)}, bf16[256,1024]{1,0:T(8,128)(2,1)}, u32[]{:S(2)}) copy-start(bf16[256,1024]{1,0:T(8,128)(2,1)} %w1_ref.1) | copy-start | bytes 1572868
  14.0 5.7 %copy-start.3 = (bf16[1024,256]{1,0:T(8,128)(2,1)S(1)}, bf16[1024,256]{1,0:T(8,128)(2,1)}, u32[]{:S(2)}) copy-start(bf16[1024,256]{1,0:T(8,128)(2,1)} %w2_ref.1) | copy-start | bytes 1572868
  19.7 18.5 %copy-start.4 = (bf16[512,512]{1,0:T(8,128)(2,1)S(1)}, bf16[512,512]{1,0:T(8,128)(2,1)}, u32[]{:S(2)}) copy-start(bf16[512,512]{1,0:T(8,128)(2,1)} %get-tuple-element.12.refs_13_) | copy-start | bytes 1572868
  19.7 18.5 %copy-start.11 = (bf16[128,512]{1,0:T(8,128)(2,1)S(1)}, bf16[128,512]{1,0:T(8,128)(2,1)}, u32[]{:S(2)}) copy-start(bf16[128,512]{1,0:T(8,128)(2,1)} %refs_16_.1) | copy-start | bytes 393220
  19.7 18.5 %copy-start.12 = (bf16[512,128]{1,0:T(8,128)(2,1)S(1)}, bf16[512,128]{1,0:T(8,128)(2,1)}, u32[]{:S(2)}) copy-start(bf16[512,128]{1,0:T(8,128)(2,1)} %refs_17_.1) | copy-start | bytes 393220
  19.7 18.5 %copy-start.16 = (bf16[128,64]{0,1:T(8,128)(2,1)S(1)}, bf16[128,64]{0,1:T(8,128)(2,1)}, u32[]{:S(2)}) copy-start(bf16[128,64]{0,1:T(8,128)(2,1)} %param.35) | copy-start | bytes 49156
  22.7 5.6 %collective-permute-start.7 = (bf16[264,128]{1,0:T(8,128)(2,1)S(1)}, bf16[264,128]{1,0:T(8,128)(2,1)S(1)}, u32[]{:S(2)}, u32[]{:S(2)}) collective-permute-start(bf16[264,128]{1,0:T(8,128)(2,1)S(1)} %get-tuple-element.11.refs_0_), channel_id=1, source_target_pairs={{0,24},{1,16},{2,8},{3,0},{4,25},{5,17},{6,9},{7,1},{8,2},{9,10},{... | collective-permute-start | bytes 202760 | tf_op jit(solution)/shard_map/ppermute | solution.py:714
  23.9 6.4 %collective-permute-start.3 = (bf16[264,128]{1,0:T(8,128)(2,1)S(1)}, bf16[264,128]{1,0:T(8,128)(2,1)S(1)}, u32[]{:S(2)}, u32[]{:S(2)}) collective-permute-start(bf16[264,128]{1,0:T(8,128)(2,1)S(1)} %get-tuple-element.11.refs_0_), channel_id=1, source_target_pairs={{0,1},{1,0},{2,3},{3,2},{4,5},{5,4},{6,7},{7,6},{8,9},{9,8},{10,11... | collective-permute-start | bytes 202760 | tf_op jit(solution)/shard_map/ppermute | solution.py:717
  23.9 7.7 %collective-permute-start.2 = (bf16[264,128]{1,0:T(8,128)(2,1)S(1)}, bf16[264,128]{1,0:T(8,128)(2,1)S(1)}, u32[]{:S(2)}, u32[]{:S(2)}) collective-permute-start(bf16[264,128]{1,0:T(8,128)(2,1)S(1)} %get-tuple-element.11.refs_0_), channel_id=1, source_target_pairs={{0,6},{1,7},{2,4},{3,5},{4,2},{5,3},{6,0},{7,1},{8,14},{9,15},{10,... | collective-permute-start | bytes 202760 | tf_op jit(solution)/shard_map/ppermute | solution.py:717
  27.2 8.8 %collective-permute-start.1 = (bf16[264,128]{1,0:T(8,128)(2,1)S(1)}, bf16[264,128]{1,0:T(8,128)(2,1)S(1)}, u32[]{:S(2)}, u32[]{:S(2)}) collective-permute-start(bf16[264,128]{1,0:T(8,128)(2,1)S(1)} %get-tuple-element.11.refs_0_), channel_id=1, source_target_pairs={{0,4},{1,5},{2,6},{3,7},{4,0},{5,1},{6,2},{7,3},{8,12},{9,13},{10,... | collective-permute-start | bytes 202760 | tf_op jit(solution)/shard_map/ppermute | solution.py:717
  27.2 8.8 %collective-permute-start = (bf16[264,128]{1,0:T(8,128)(2,1)S(1)}, bf16[264,128]{1,0:T(8,128)(2,1)S(1)}, u32[]{:S(2)}, u32[]{:S(2)}) collective-permute-start(bf16[264,128]{1,0:T(8,128)(2,1)S(1)} %get-tuple-element.11.refs_0_), channel_id=1, source_target_pairs={{0,2},{1,3},{2,0},{3,1},{4,6},{5,7},{6,4},{7,5},{8,10},{9,11},{10,... | collective-permute-start | bytes 202760 | tf_op jit(solution)/shard_map/ppermute | solution.py:717
  28.3 8.2 %collective-permute-start.10 = (bf16[264,128]{1,0:T(8,128)(2,1)S(1)}, bf16[264,128]{1,0:T(8,128)(2,1)S(1)}, u32[]{:S(2)}, u32[]{:S(2)}) collective-permute-start(bf16[264,128]{1,0:T(8,128)(2,1)S(1)} %collective-permute-done.7.refs_8_), channel_id=1, source_target_pairs={{0,24},{8,16},{16,8},{24,0},{1,25},{9,17},{17,9},{25,1},{2,26},{10... | collective-permute-start | bytes 202760 | tf_op jit(solution)/shard_map/ppermute | solution.py:720
  30.4 7.8 %collective-permute-start.9 = (bf16[264,128]{1,0:T(8,128)(2,1)S(1)}, bf16[264,128]{1,0:T(8,128)(2,1)S(1)}, u32[]{:S(2)}, u32[]{:S(2)}) collective-permute-start(bf16[264,128]{1,0:T(8,128)(2,1)S(1)} %collective-permute-done.7.refs_8_), channel_id=1, source_target_pairs={{0,16},{8,24},{16,0},{24,8},{1,17},{9,25},{17,1},{25,9},{2,18},{10... | collective-permute-start | bytes 202760 | tf_op jit(solution)/shard_map/ppermute | solution.py:720
  31.6 6.6 %collective-permute-start.8 = (bf16[264,128]{1,0:T(8,128)(2,1)S(1)}, bf16[264,128]{1,0:T(8,128)(2,1)S(1)}, u32[]{:S(2)}, u32[]{:S(2)}) collective-permute-start(bf16[264,128]{1,0:T(8,128)(2,1)S(1)} %collective-permute-done.7.refs_8_), channel_id=1, source_target_pairs={{0,8},{8,0},{16,24},{24,16},{1,9},{9,1},{17,25},{25,17},{2,10},{10... | collective-permute-start | bytes 202760 | tf_op jit(solution)/shard_map/ppermute | solution.py:720
  36.0 2.2 %collective-permute-start.6 = (bf16[264,128]{1,0:T(8,128)(2,1)S(1)}, bf16[264,128]{1,0:T(8,128)(2,1)S(1)}, u32[]{:S(2)}, u32[]{:S(2)}) collective-permute-start(bf16[264,128]{1,0:T(8,128)(2,1)S(1)} %collective-permute-done.2.refs_3_), channel_id=1, source_target_pairs={{0,1},{1,0},{2,3},{3,2},{4,5},{5,4},{6,7},{7,6},{8,9},{9,8},{10,11... | collective-permute-start | bytes 202760 | tf_op jit(solution)/shard_map/ppermute | solution.py:717
  36.0 2.2 %collective-permute-start.5 = (bf16[264,128]{1,0:T(8,128)(2,1)S(1)}, bf16[264,128]{1,0:T(8,128)(2,1)S(1)}, u32[]{:S(2)}, u32[]{:S(2)}) collective-permute-start(bf16[264,128]{1,0:T(8,128)(2,1)S(1)} %collective-permute-done.1.refs_2_), channel_id=1, source_target_pairs={{0,1},{1,0},{2,3},{3,2},{4,5},{5,4},{6,7},{7,6},{8,9},{9,8},{10,11... | collective-permute-start | bytes 202760 | tf_op jit(solution)/shard_map/ppermute | solution.py:717
  36.5 1.7 %collective-permute-start.4 = (bf16[264,128]{1,0:T(8,128)(2,1)S(1)}, bf16[264,128]{1,0:T(8,128)(2,1)S(1)}, u32[]{:S(2)}, u32[]{:S(2)}) collective-permute-start(bf16[264,128]{1,0:T(8,128)(2,1)S(1)} %collective-permute-done.refs_1_), channel_id=1, source_target_pairs={{0,1},{1,0},{2,3},{3,2},{4,5},{5,4},{6,7},{7,6},{8,9},{9,8},{10,11... | collective-permute-start | bytes 202760 | tf_op jit(solution)/shard_map/ppermute | solution.py:717
  37.3 1.0 %copy-start = (bf16[1024,128]{1,0:T(8,128)(2,1)S(1)}, bf16[1024,128]{1,0:T(8,128)(2,1)}, u32[]{:S(2)}) copy-start(bf16[1024,128]{1,0:T(8,128)(2,1)} %turn.1._.refs_15_) | copy-start | bytes 786436
  37.3 1.0 %copy-start.1 = (bf16[1024,128]{1,0:T(8,128)(2,1)S(1)}, bf16[1024,128]{1,0:T(8,128)(2,1)}, u32[]{:S(2)}) copy-start(bf16[1024,128]{1,0:T(8,128)(2,1)} %get-tuple-element.9._2.refs_12_) | copy-start | bytes 786436
